TPU v7x, 32 devices: a whole 2x2x4 slice. The times are simulated.
32 devices in a mesh: tower: 2 (over core), batch: 16 (over z, y, x).
Axes of the slice: x: 2, y: 2, z: 4, core: 2. Of those that a mesh axis runs over, the one named last changes fastest.
Arguments:
- shard_ids: int32 [3, 1664, 10, 8], P(None, 'batch'), may hold values from 0 to 31, all different within a row; in each aligned block of 1040 rows (0 to 1039, 1040 to 2079, ..., all dimensions but the last counted through in order) at most 1040 rows name the same one
- local_rows: int32 [3, 1664, 10, 8], P(None, 'batch'), may hold values from 0 to 32767
- bag_counts: int32 [3, 1664, 39], P(None, 'batch'), may hold values from 1 to 24, 80 in all within a row
- click_labels: int32 [3, 1664], P(None, 'batch'), may hold values 0 or 1
- sample_weights: int32 [3, 1664], P(None, 'batch'), may hold values from 1 to 5
- embed_table: float32 [11, 1048576], P(None, ('tower', 'batch')), may hold values from -1 to 1
- table_first: float32 [11, 1048576], P(None, ('tower', 'batch')), may hold values from -1 to 1
- table_second: float32 [11, 1048576], P(None, ('tower', 'batch')), may hold values from 0 to 1
- dense_params: float32 [621632], P(('tower', 'batch')), may hold values from -1.5 to 1.5
- dense_first: float32 [621632], P(('tower', 'batch')), may hold values from -1 to 1
- dense_second: float32 [621632], P(('tower', 'batch')), may hold values from 0 to 1
Outputs:
- table_new: float32 [11, 1048576], P(None, ('tower', 'batch'))
- table_first_new: float32 [11, 1048576], P(None, ('tower', 'batch'))
- table_second_new: float32 [11, 1048576], P(None, ('tower', 'batch'))
- table_copy: bfloat16 [11, 1048576], P(None, ('tower', 'batch'))
- dense_new: float32 [621632], P(('tower', 'batch'))
- dense_first_new: float32 [621632], P(('tower', 'batch'))
- dense_second_new: float32 [621632], P(('tower', 'batch'))
- dense_copy: bfloat16 [621632], P(('tower', 'batch'))
- loss_value: float32 [], replicated
Inputs may be any that keep to these rules, and one draw needn't show every extreme that they name: `shard_ids`: within each group of 8 the shards differ; over the ids of one device's samples in one micro-batch (aligned blocks of 104 samples) no shard is named more than 1040 times, a bound that some block reaches. `bag_counts`: the 39 counts of each sample add up to 80.
All inputs are finite; a program needn't handle non-finite values. No bound on the sum of `click_labels` on one device may be relied on, other than what follows from the above.
Results may differ from a plain program's by a relative error of at most 0.004.
The roundings to bfloat16 on the way count: a program that leaves them out, or rounds other values in their place, can miss the bound.
Values may be sent and summed in bfloat16 or wider, within the bound.
A program may use at most 192 MiB of HBM per device.

v0:
```python
from functools import partial

import jax
import jax.numpy as jnp
from jax import lax
from jax.experimental import pallas as pl
from jax.experimental.pallas import tpu as pltpu
from jax.sharding import PartitionSpec as P

FIELDS = 39
EMB = 10
MAPS = 200
HID = 400
IDS_SAMP = 80

beta_one = 0.9
beta_two = 0.999
epsilon = 1e-08
decay_rate = 0.15
rate_table = 0.1
rate_dense = 0.05
step_count = 10

LANES = 128
WIDE = 256
BROAD = 512
TALL = 64
HALF = 24
BAG_ROWS = EMB * HALF + 8
FPAD = 40
PAIRS = FIELDS * FPAD
SQUARE = FIELDS * FIELDS
CIN_SIZE = MAPS * SQUARE + MAPS
FLAT = EMB * FIELDS
B_ONE, W_TWO, B_TWO, W_THREE, BIAS = FLAT, FLAT + 1, FLAT + HID + 1, FLAT + HID + 2, FLAT + HID + 3
HPAD = 512
PLANE = 4
NT = (((1,), (1,)), ((), ()))
TN = (((0,), (0,)), ((), ()))
NN = (((1,), (0,)), ((), ()))


def adam_update(weight, first_old, second_old, gradient, step_rate):
    first_new = beta_one * first_old + (1.0 - beta_one) * gradient
    second_new = beta_two * second_old + (1.0 - beta_two) * gradient * gradient
    first_hat = first_new / (1.0 - beta_one**step_count)
    second_hat = second_new / (1.0 - beta_two**step_count)
    weight_new = weight - step_rate * (
        first_hat / (jnp.sqrt(second_hat) + epsilon) + decay_rate * weight
    )
    return (weight_new, first_new, second_new)


def dot(a, b, dims=NN):
    return lax.dot_general(a, b, dims, preferred_element_type=jnp.float32)


def iota(shape, dim):
    return lax.broadcasted_iota(jnp.int32, shape, dim)


def ones_at(mask):
    return jnp.where(mask, 1.0, 0.0).astype(jnp.bfloat16)


def layout_of(micro_count, capacity, size=WIDE):
    first_rows = [m * capacity // size for m in range(micro_count)]
    shifts = [m * capacity % size for m in range(micro_count)]
    window = max(-(-(shift + capacity) // WIDE) for shift in shifts)
    return first_rows, shifts, window, max(first_rows) + window


class Windows:
    def __init__(self, share, batch_count):
        self.share, self.batch_count = share, batch_count
        self.cin_rows = -(-(SQUARE - 1 + share) // SQUARE)
        self.rest_rows = -(-(HID - 1 + share) // HID)
        self.cin_pad = -(-self.cin_rows // 16) * 16
        self.rest_pad = -(-self.rest_rows // 16) * 16
        self.first_extra = CIN_SIZE // share
        self.extras = batch_count - self.first_extra
        self.cin_at = [b * share // SQUARE for b in range(batch_count)]
        self.rest_at = [
            ((batch_count + b) * share - CIN_SIZE) // HID for b in range(batch_count)
        ]
        self.extra_at = [
            (b * share - CIN_SIZE) // HID for b in range(self.first_extra, batch_count)
        ]
        depth = batch_count // PLANE
        self.slots = [b % PLANE * depth + b // PLANE for b in range(batch_count)]
        self.cin_total = -(-max(a + self.cin_rows for a in self.cin_at) // 8) * 8
        self.rest_total = -(-max(a + self.rest_rows for a in self.rest_at) // 8) * 8

    def phases(self, device):
        start = device * self.share
        return start % SQUARE, jnp.mod(start - CIN_SIZE, HID)


def bf16_iota(rows, width):
    return iota((rows, width), 0).astype(jnp.float32).astype(jnp.bfloat16)


def route_kernel(
    capacity, batch_count, micro_count, ids_ref, rows_ref, counts_ref,
    req_ref, code_ref, half_ref, part_ref, left_ref, right_ref,
):
    f32, bf16 = jnp.float32, jnp.bfloat16
    first_rows, shifts, window, _ = layout_of(micro_count, capacity, 2 * WIDE)
    rows_msg = req_ref.shape[1]
    micro = pl.program_id(0)
    id_rows, samples = ids_ref.shape[1:]
    chunk = 16
    tower = lax.axis_index("tower")

    @pl.when(micro == 0)
    def _():
        req_ref[...] = jnp.zeros_like(req_ref)
        code_ref[...] = jnp.zeros_like(code_ref)
        half_ref[...] = jnp.zeros_like(half_ref)
        part_ref[...] = jnp.zeros_like(part_ref)

    def widened(x, filler):
        part_ref[0, :, :samples] = x.astype(f32)
        inside = iota((id_rows, LANES), 1) < samples
        return jnp.where(inside, part_ref[0], filler)

    owner = ids_ref[0]
    target = widened(
        jnp.where(owner // batch_count == tower, owner % batch_count, batch_count), batch_count
    ).astype(jnp.int32)
    local = widened(rows_ref[0], 0.0).astype(jnp.int32)
    before = ones_at(iota((FIELDS, FIELDS), 1) <= iota((FIELDS, FIELDS), 0))
    ends = dot(before, counts_ref[0].astype(f32).astype(bf16)).astype(jnp.int32)
    field = jnp.zeros((id_rows, samples), jnp.int32)
    for f in range(FIELDS):
        field = field + jnp.where(iota((id_rows, samples), 0) >= ends[f : f + 1], 1, 0)
    field = widened(field, 0.0)
    late = jnp.where(field >= HALF, 1.0, 0.0)

    earlier_rows = ones_at(iota((id_rows, id_rows), 1) < iota((id_rows, id_rows), 0))
    upper = iota((2 * LANES, LANES), 0)
    mixing = ones_at((upper < iota((2 * LANES, LANES), 1)) | (upper >= LANES))
    rank = jnp.zeros((id_rows, LANES), f32)
    for begin in range(0, batch_count, chunk):
        hots = [ones_at(target == begin + d) for d in range(chunk)]
        above = dot(earlier_rows, jnp.concatenate(hots, axis=1)).astype(bf16)
        stacked = jnp.concatenate(
            [
                jnp.concatenate([hots[d], above[:, d * LANES : (d + 1) * LANES]], axis=1)
                for d in range(chunk)
            ],
            axis=0,
        )
        ranks = dot(stacked, mixing)
        for d in range(chunk):
            rank = rank + jnp.where(
                target == begin + d, ranks[d * id_rows : (d + 1) * id_rows], 0.0
            )
    shift = sum(jnp.where(micro == m, shifts[m], 0) for m in range(micro_count))
    slot = rank.astype(jnp.int32) + shift
    lane = slot % (2 * WIDE)
    place = jnp.where(target < batch_count, (slot // (2 * WIDE)) * batch_count + target, -1)
    part_ref[0] = place.astype(f32)
    part_ref[1] = jnp.where(lane < WIDE, lane, -1).astype(f32)
    part_ref[2] = jnp.where(lane < WIDE, -1, lane - WIDE).astype(f32)
    part_ref[3] = (local // WIDE).astype(f32)
    part_ref[4] = (local % WIDE).astype(f32)
    part_ref[5] = late * LANES + (iota((id_rows, LANES), 1) + 1).astype(f32)
    part_ref[6] = field - late * HALF
    places = window * batch_count
    one, zero = jnp.ones((), bf16), jnp.zeros((), bf16)

    def build(t, carry):
        span = pl.ds(pl.multiple_of(t * LANES, LANES), LANES)

        def row(k):
            return part_ref[k, pl.ds(t, 1), :].astype(bf16)

        mask = bf16_iota(places, LANES) == row(0)
        for v in range(4):
            left_ref[v * places : (v + 1) * places, span] = jnp.where(mask, row(3 + v), zero)
        for h in range(2):
            right_ref[h * WIDE : (h + 1) * WIDE, span] = jnp.where(
                bf16_iota(WIDE, LANES) == row(1 + h), one, zero
            )
        return carry

    lax.fori_loop(0, id_rows, build, 0, unroll=4)
    placed = dot(left_ref[...], right_ref[...], NT).astype(jnp.int32)

    def part(v, r, h):
        begin = (v * window + r) * batch_count
        return placed[begin : begin + batch_count, h * WIDE : (h + 1) * WIDE]

    for m in range(micro_count):

        @pl.when(micro == m)
        def _():
            for r in range(window):
                for h in range(2):
                    at = 2 * (first_rows[m] + r) + h
                    if at < rows_msg:
                        code = part(2, r, h)
                        req_ref[:, at, :] += part(0, r, h) * WIDE + part(1, r, h)
                        code_ref[:, at, :] += jnp.where(code > 0, code + m * WIDE, 0)
                        half_ref[:, at, :] += part(3, r, h)


def route(ids, rows, counts, capacity, batch_count):
    micro_count, id_rows, samples = ids.shape
    rows_msg = layout_of(micro_count, capacity)[3]
    places = layout_of(micro_count, capacity, 2 * WIDE)[2] * batch_count

    def block(x):
        return pl.BlockSpec((1,) + x.shape[1:], lambda m: (m, 0, 0))

    whole = pl.BlockSpec((batch_count, rows_msg, WIDE), lambda m: (0, 0, 0))
    shape = jax.ShapeDtypeStruct((batch_count, rows_msg, WIDE), jnp.int32)
    return pl.pallas_call(
        partial(route_kernel, capacity, batch_count, micro_count),
        grid=(micro_count,),
        in_specs=[block(ids), block(rows), block(counts)],
        out_specs=[whole] * 3,
        out_shape=[shape] * 3,
        scratch_shapes=[
            pltpu.VMEM((7, id_rows, LANES), jnp.float32),
            pltpu.VMEM((4 * places, id_rows * LANES), jnp.bfloat16),
            pltpu.VMEM((2 * WIDE, id_rows * LANES), jnp.bfloat16),
        ],
        compiler_params=pltpu.CompilerParams(vmem_limit_bytes=60 << 20),
        name="route",
    )(ids, rows, counts)


def peer_copy(src, dst, send_sem, recv_sem, peer):
    return pltpu.make_async_remote_copy(
        src_ref=src,
        dst_ref=dst,
        send_sem=send_sem,
        recv_sem=recv_sem,
        device_id={"batch": peer},
        device_id_type=pl.DeviceIdType.MESH,
    )


def greet(me, batch_count, other_tower=None):
    barrier = pltpu.get_barrier_semaphore()

    def signal(i, carry):
        pl.semaphore_signal(
            barrier,
            inc=1,
            device_id={"batch": lax.rem(me + i, batch_count)},
            device_id_type=pl.DeviceIdType.MESH,
        )
        return carry

    lax.fori_loop(1, batch_count, signal, 0)
    if other_tower is not None:
        pl.semaphore_signal(
            barrier,
            inc=1,
            device_id={"tower": other_tower},
            device_id_type=pl.DeviceIdType.MESH,
        )
    pl.semaphore_wait(barrier, batch_count - (1 if other_tower is None else 0))


def message_rows(rows_msg, columns):
    return -(-rows_msg * columns // 16) * 16


def each(count, action):
    def body(i, carry):
        action(i)
        return carry

    lax.fori_loop(1, count, body, 0)


def pick_rows(result, mask, depth, columns):
    width = result.shape[1]
    out = jnp.zeros((16, width), jnp.float32)
    for c in range(columns):
        row = jnp.sum(
            jnp.where(mask, result[c * depth : (c + 1) * depth], 0.0), axis=0, keepdims=True
        )
        out = jnp.where(iota((16, width), 0) == c, row, out)
    return out


def tile_table(table_ref, tiles_ref, stage_ref, columns):
    for c in range(columns):
        for q in range(TALL):
            stage_ref[q : q + 1, :] = table_ref[c : c + 1, q * BROAD : (q + 1) * BROAD]
        tiles_ref[c * TALL : (c + 1) * TALL, :] = stage_ref[...].astype(jnp.bfloat16)


def fetch_kernel(
    capacity, micro_count, windows, columns,
    req_ref, code_ref, half_ref, table_ref, weight_ref, cin_ref, rest_ref,
    out_ref, served_ref, stat_out_ref, cins_ref, rests_ref, extras_ref,
    tiles_ref, stage_ref, first_ref, second_ref, ans_out_ref, ans_in_ref, left_ref, pooled_ref,
    other_ref, stat_ref, stat_in_ref,
    req_send, req_recv, ans_send, ans_recv, stat_send, stat_recv, win_send, win_recv, plane_send,
    plane_recv, ext_send, ext_recv, pair_send, pair_recv,
):
    first_rows, _, window, rows_msg = layout_of(micro_count, capacity)
    batch_count = windows.batch_count
    first_extra = windows.first_extra
    me = lax.axis_index("batch")
    tower = lax.axis_index("tower")
    other_tower = 1 - tower
    greet(me, batch_count, other_tower)

    def request_copy(peer, slot):
        return peer_copy(
            req_ref.at[peer], served_ref.at[slot], req_send.at[peer], req_recv.at[slot], peer
        )

    stat_ref[...] = jnp.full(stat_ref.shape, jnp.sum(weight_ref[...].astype(jnp.float32)))

    def stat_copy(peer, slot):
        return peer_copy(stat_ref, stat_in_ref.at[slot], stat_send.at[peer], stat_recv.at[slot], peer)

    def answer_copy(peer, slot):
        return peer_copy(
            ans_out_ref.at[peer], ans_in_ref.at[slot], ans_send.at[peer], ans_recv.at[slot], peer
        )

    def own_copy():
        return pltpu.make_async_copy(ans_out_ref.at[me], ans_in_ref.at[me], ans_recv.at[me])

    def send_requests(i, carry):
        peer = lax.rem(me + i, batch_count)
        request_copy(peer, me).start()
        stat_copy(peer, me).start()
        return carry

    lax.fori_loop(1, batch_count, send_requests, 0)

    depth = batch_count // PLANE
    high, low = me // PLANE, lax.rem(me, PLANE)

    def others(action):
        each(batch_count, lambda i: action(lax.rem(me + i, batch_count)))

    def column(action):
        each(depth, lambda i: action(lax.rem(high + i, depth)))

    def plane(action):
        each(PLANE, lambda i: action(lax.rem(low + i, PLANE)))

    def column_copy(src, dst, to, source):
        return peer_copy(
            src, dst.at[low * depth + source], win_send.at[to], win_recv.at[source],
            to * PLANE + low,
        )

    def plane_copy(dst, to, source):
        block = dst.at[pl.ds(source * depth, depth)]
        return peer_copy(
            block, block, plane_send.at[to], plane_recv.at[source], high * PLANE + to
        )

    def extra_copy(peer, slot):
        return peer_copy(rest_ref, extras_ref.at[slot], ext_send.at[peer], ext_recv.at[slot], peer)

    def start_windows(src, dst):
        column(lambda to: column_copy(src, dst, to, high).start())
        dst[low * depth + high] = src[...]

    def pass_windows(src, dst):
        column(lambda source: column_copy(src, dst, source, source).wait_recv())
        plane(lambda to: plane_copy(dst, to, low).start())

    def sent_windows(src, dst):
        column(lambda to: column_copy(src, dst, to, high).wait_send())
        plane(lambda to: plane_copy(dst, to, low).wait_send())

    def split(action):
        @pl.when(tower == 0)
        def _():
            action(cin_ref, cins_ref)

        @pl.when(tower == 1)
        def _():
            action(rest_ref, rests_ref)

    served_ref[me] = req_ref[me]
    stat_in_ref[me] = stat_ref[...]
    tile_table(table_ref, tiles_ref, stage_ref, columns)
    pooled_ref[...] = jnp.zeros_like(pooled_ref)

    sizes = ans_out_ref.shape[1]

    def look_up(first, second):
        for r in range(rows_msg):
            row = jnp.concatenate(
                [served_ref[first, r : r + 1, :], served_ref[second, r : r + 1, :]], axis=1
            )
            hot = ones_at(iota((BROAD, 2 * WIDE), 0) == row % BROAD)
            result = dot(tiles_ref[...], hot)
            mask = iota((TALL, 2 * WIDE), 0) == row // BROAD
            block = pick_rows(result, mask, TALL, columns)
            first_ref[r * columns : r * columns + 16, :] = block[:, :WIDE]
            second_ref[r * columns : r * columns + 16, :] = block[:, WIDE:]
        ans_out_ref[first] = first_ref[:sizes, :].astype(jnp.bfloat16)
        ans_out_ref[second] = second_ref[:sizes, :].astype(jnp.bfloat16)

    def pool(owner):
        first_ref[:sizes, :] = ans_in_ref[owner].astype(jnp.float32)
        for r in range(rows_msg):
            span = slice(r * WIDE, (r + 1) * WIDE)
            values = [first_ref[r * columns + c : r * columns + c + 1, :] for c in range(columns)]
            mask = iota((HALF, WIDE), 0) == half_ref[owner, r : r + 1, :]
            pieces = [jnp.where(mask, values[c], 0.0) for c in range(EMB)]
            pieces.append(jnp.where(iota((8, WIDE), 0) == 0, values[EMB], 0.0))
            left_ref[:, span] = jnp.concatenate(pieces, axis=0).astype(jnp.bfloat16)
        for m in range(micro_count):
            rights = [
                ones_at(iota((WIDE, WIDE), 0) + (m * WIDE + 1) == code_ref[owner, r : r + 1, :])
                for r in range(first_rows[m], first_rows[m] + window)
            ]
            span = slice(first_rows[m] * WIDE, (first_rows[m] + window) * WIDE)
            pooled_ref[m] += dot(left_ref[:, span], jnp.concatenate(rights, axis=1), NT)

    pairs = batch_count // 2
    lag = 2

    def step(j, carry):
        @pl.when(j < pairs)
        def _():
            first = lax.rem(me + batch_count - (2 * j + 1), batch_count)
            second = lax.rem(me + 2 * batch_count - (2 * j + 2), batch_count)
            request_copy(first, first).wait_recv()

            @pl.when(j < pairs - 1)
            def _():
                request_copy(second, second).wait_recv()

            look_up(first, second)

            @pl.when(j == 0)
            def _():
                split(start_windows)

            @pl.when((j == 0) & (tower == 0) & (me >= first_extra))
            def _():
                others(lambda peer: extra_copy(peer, me - first_extra).start())
                extras_ref[me - first_extra] = rest_ref[...]

            @pl.when(j == 3)
            def _():
                split(pass_windows)

            answer_copy(first, me).start()

            @pl.when(j < pairs - 1)
            def _():
                answer_copy(second, me).start()

            @pl.when(j == pairs - 1)
            def _():
                own_copy().start()

        @pl.when(j >= lag)
        def _():
            first = lax.rem(me + 2 * (j - lag) + 1, batch_count)
            answer_copy(first, first).wait_recv()
            pool(first)

        @pl.when((j >= lag) & (j < pairs - 1 + lag))
        def _():
            second = lax.rem(me + 2 * (j - lag) + 2, batch_count)
            answer_copy(second, second).wait_recv()
            pool(second)

        return carry

    lax.fori_loop(0, pairs + lag, step, 0)

    def pair_copy(src, dst, k):
        return pltpu.make_async_remote_copy(
            src_ref=src,
            dst_ref=dst,
            send_sem=pair_send.at[k],
            recv_sem=pair_recv.at[k],
            device_id={"tower": other_tower},
            device_id_type=pl.DeviceIdType.MESH,
        )

    @pl.when(tower == 0)
    def _():
        plane(lambda source: plane_copy(cins_ref, source, source).wait_recv())
        for e in range(windows.extras):

            @pl.when(me != first_extra + e)
            def _():
                extra_copy(first_extra + e, e).wait_recv()

        pair_copy(cins_ref, cins_ref, 0).start()
        pair_copy(extras_ref, extras_ref, 1).start()

    @pl.when(tower == 1)
    def _():
        plane(lambda source: plane_copy(rests_ref, source, source).wait_recv())
        pair_copy(rests_ref, rests_ref, 0).start()

    own_copy().wait()
    pool(me)

    pooled_pair = pair_copy(pooled_ref, other_ref, 2)
    pooled_pair.start()

    def finish(i, carry):
        peer = lax.rem(me + i, batch_count)
        request_copy(peer, me).wait_send()
        stat_copy(peer, me).wait_send()
        answer_copy(peer, me).wait_send()
        stat_copy(peer, peer).wait_recv()
        return carry

    lax.fori_loop(1, batch_count, finish, 0)
    stat_out_ref[...] = jnp.sum(stat_in_ref[...], axis=0)

    split(sent_windows)

    @pl.when(tower == 0)
    def _():
        @pl.when(me >= first_extra)
        def _():
            others(lambda peer: extra_copy(peer, me - first_extra).wait_send())

        pair_copy(cins_ref, cins_ref, 0).wait_send()
        pair_copy(extras_ref, extras_ref, 1).wait_send()
        pair_copy(rests_ref, rests_ref, 0).wait_recv()

    @pl.when(tower == 1)
    def _():
        pair_copy(rests_ref, rests_ref, 0).wait_send()
        pair_copy(cins_ref, cins_ref, 0).wait_recv()
        pair_copy(extras_ref, extras_ref, 1).wait_recv()

    pooled_pair.wait()
    out_ref[...] = pooled_ref[...] + other_ref[...]


def fetch(
    requests, codes, halves, table, weights, cin_window, rest_window, windows, capacity, micro_count
):
    batch_count, rows_msg, _ = requests.shape
    columns, rows_dev = table.shape
    slots = rows_msg * WIDE
    sizes = message_rows(rows_msg, columns)
    in_vmem = pl.BlockSpec(memory_space=pltpu.VMEM)
    dma = pltpu.SemaphoreType.DMA
    bags = (micro_count, BAG_ROWS, WIDE)
    return pl.pallas_call(
        partial(fetch_kernel, capacity, micro_count, windows, columns),
        in_specs=[in_vmem] * 7,
        out_specs=[in_vmem] * 6,
        out_shape=[
            jax.ShapeDtypeStruct(bags, jnp.float32),
            jax.ShapeDtypeStruct(requests.shape, jnp.int32),
            jax.ShapeDtypeStruct((8, LANES), jnp.float32),
            jax.ShapeDtypeStruct((batch_count,) + cin_window.shape, jnp.bfloat16),
            jax.ShapeDtypeStruct((batch_count,) + rest_window.shape, jnp.bfloat16),
            jax.ShapeDtypeStruct((windows.extras,) + rest_window.shape, jnp.bfloat16),
        ],
        scratch_shapes=[
            pltpu.VMEM((columns * TALL, BROAD), jnp.bfloat16),
            pltpu.VMEM((TALL, BROAD), jnp.float32),
            pltpu.VMEM((sizes + 16, WIDE), jnp.float32),
            pltpu.VMEM((sizes + 16, WIDE), jnp.float32),
            pltpu.VMEM((batch_count, sizes, WIDE), jnp.bfloat16),
            pltpu.VMEM((batch_count, sizes, WIDE), jnp.bfloat16),
            pltpu.VMEM((BAG_ROWS, slots), jnp.bfloat16),
            pltpu.VMEM(bags, jnp.float32),
            pltpu.VMEM(bags, jnp.float32),
            pltpu.VMEM((8, LANES), jnp.float32),
            pltpu.VMEM((batch_count, 8, LANES), jnp.float32),
        ]
        + [dma((batch_count,))] * 11
        + [dma((windows.extras,)), dma((3,)), dma((3,))],
        compiler_params=pltpu.CompilerParams(
            vmem_limit_bytes=60 << 20, collective_id=0, has_side_effects=True
        ),
        name="fetch",
    )(requests, codes, halves, table, weights, cin_window, rest_window)


def return_kernel(
    capacity, micro_count, windows, columns,
    grad_ref, code_ref, half_ref, served_ref, stat_ref, cins_ref, rests_ref, extras_ref,
    out_ref, stat_out_ref, cin_ref, rest_ref,
    send_ref, recv_ref, first_ref, second_ref, left_ref, right_ref, total_ref, stat_in_ref,
    extra_in_ref, cin_near_ref, cin_sum_ref, cin_far_ref, rest_near_ref, rest_sum_ref, rest_far_ref,
    val_send, val_recv, stat_send, stat_recv, win_send, win_recv, plane_send, plane_recv, ext_send,
    ext_recv,
):
    batch_count = windows.batch_count
    first_extra = windows.first_extra
    tower = lax.axis_index("tower")
    first_rows, _, window, rows_msg = layout_of(micro_count, capacity)
    me = lax.axis_index("batch")
    greet(me, batch_count)

    def value_copy(peer, slot):
        return peer_copy(
            send_ref.at[peer], recv_ref.at[slot], val_send.at[peer], val_recv.at[slot], peer
        )

    def own_copy():
        return pltpu.make_async_copy(send_ref.at[me], recv_ref.at[me], val_recv.at[me])

    def stat_copy(peer, slot):
        return peer_copy(stat_ref, stat_in_ref.at[slot], stat_send.at[peer], stat_recv.at[slot], peer)

    depth = batch_count // PLANE
    high, low = me // PLANE, lax.rem(me, PLANE)

    def others(action):
        each(batch_count, lambda i: action(lax.rem(me + i, batch_count)))

    def column(action):
        each(depth, lambda i: action(lax.rem(high + i, depth)))

    def plane(action):
        each(PLANE, lambda i: action(lax.rem(low + i, PLANE)))

    def plane_copy(src, near, to, source):
        return peer_copy(
            src.at[pl.ds(to * depth, depth)], near.at[source], plane_send.at[to],
            plane_recv.at[source], high * PLANE + to,
        )

    def column_copy(total, far, to, source):
        return peer_copy(
            total.at[to], far.at[source], win_send.at[to], win_recv.at[source], to * PLANE + low
        )

    def start_windows(src, near, total, far, out):
        plane(lambda to: plane_copy(src, near, to, low).start())
        near[low] = src[pl.ds(low * depth, depth)]

    def pass_windows(src, near, total, far, out):
        plane(lambda source: plane_copy(src, near, source, source).wait_recv())
        total[...] = jnp.sum(near[...], axis=0)
        column(lambda to: column_copy(total, far, to, high).start())
        far[high] = total[high]

    def end_windows(src, near, total, far, out):
        column(lambda source: column_copy(total, far, source, source).wait_recv())
        out[...] = jnp.sum(far[...], axis=0)
        plane(lambda to: plane_copy(src, near, to, low).wait_send())
        column(lambda to: column_copy(total, far, to, high).wait_send())

    def split(action):
        @pl.when(tower == 0)
        def _():
            action(cins_ref, cin_near_ref, cin_sum_ref, cin_far_ref, cin_ref)

        @pl.when(tower == 1)
        def _():
            action(rests_ref, rest_near_ref, rest_sum_ref, rest_far_ref, rest_ref)

    def extra_copy(peer, slot):
        return peer_copy(
            extras_ref.at[peer - first_extra],
            extra_in_ref.at[slot],
            ext_send.at[peer],
            ext_recv.at[slot],
            peer,
        )

    def send_stats(i, carry):
        stat_copy(lax.rem(me + i, batch_count), me).start()
        return carry

    lax.fori_loop(1, batch_count, send_stats, 0)
    stat_in_ref[me] = stat_ref[...]
    total_ref[...] = jnp.zeros_like(total_ref)

    sizes = send_ref.shape[1]

    def spread(first, second):
        for r in range(rows_msg):
            code = jnp.concatenate(
                [code_ref[first, r : r + 1, :], code_ref[second, r : r + 1, :]], axis=1
            )
            half = jnp.concatenate(
                [half_ref[first, r : r + 1, :], half_ref[second, r : r + 1, :]], axis=1
            )
            result = None
            for m in range(micro_count):
                if first_rows[m] <= r < first_rows[m] + window:
                    hot = ones_at(iota((WIDE, 2 * WIDE), 0) + (m * WIDE + 1) == code)
                    found = dot(grad_ref[m], hot)
                    result = found if result is None else result + found
            block = pick_rows(result, iota((HALF, 2 * WIDE), 0) == half, HALF, EMB)
            linear = result[EMB * HALF : EMB * HALF + 1]
            block = jnp.where(iota((16, 2 * WIDE), 0) == EMB, linear, block)
            first_ref[r * columns : r * columns + 16, :] = block[:, :WIDE]
            second_ref[r * columns : r * columns + 16, :] = block[:, WIDE:]
        send_ref[first] = first_ref[:sizes, :].astype(jnp.bfloat16)
        send_ref[second] = second_ref[:sizes, :].astype(jnp.bfloat16)

    def scatter(source):
        first_ref[:sizes, :] = recv_ref[source].astype(jnp.float32)
        for r in range(rows_msg):
            span = slice(r * WIDE, (r + 1) * WIDE)
            row = served_ref[source, r : r + 1, :]
            mask = iota((TALL, WIDE), 0) == row // BROAD
            for c in range(columns):
                left_ref[c * TALL : (c + 1) * TALL, span] = jnp.where(
                    mask, first_ref[r * columns + c : r * columns + c + 1, :], 0.0
                ).astype(jnp.bfloat16)
            right_ref[:, span] = ones_at(iota((BROAD, WIDE), 0) == row % BROAD)
        total_ref[...] += dot(left_ref[...], right_ref[...], NT)

    pairs = batch_count // 2
    lag = 2

    def step(j, carry):
        @pl.when(j < pairs)
        def _():
            first = lax.rem(me + 2 * j + 1, batch_count)
            second = lax.rem(me + 2 * j + 2, batch_count)
            spread(first, second)
            value_copy(first, me).start()

            @pl.when(j == 1)
            def _():
                split(start_windows)

            @pl.when((j == 1) & (tower == 0))
            def _():
                for e in range(windows.extras):

                    @pl.when(me != first_extra + e)
                    def _():
                        extra_copy(first_extra + e, me).start()

            @pl.when(j < pairs - 1)
            def _():
                value_copy(second, me).start()

            @pl.when(j == pairs - 1)
            def _():
                own_copy().start()

        @pl.when(j == pairs - 1)
        def _():
            split(pass_windows)

        @pl.when(j >= lag)
        def _():
            first = lax.rem(me + batch_count - (2 * (j - lag) + 1), batch_count)
            value_copy(first, first).wait_recv()
            scatter(first)

        @pl.when((j >= lag) & (j < pairs - 1 + lag))
        def _():
            second = lax.rem(me + 2 * batch_count - (2 * (j - lag) + 2), batch_count)
            value_copy(second, second).wait_recv()
            scatter(second)

        return carry

    lax.fori_loop(0, pairs + lag, step, 0)
    own_copy().wait()
    scatter(me)

    split(end_windows)

    @pl.when(tower == 0)
    def _():
        for e in range(windows.extras):

            @pl.when(me != first_extra + e)
            def _():
                extra_copy(first_extra + e, me).wait_send()

        @pl.when(me >= first_extra)
        def _():
            extra_in_ref[me] = extras_ref[me - first_extra]
            others(lambda peer: extra_copy(me, peer).wait_recv())
            rest_ref[...] = jnp.sum(extra_in_ref[...], axis=0)

        @pl.when(me < first_extra)
        def _():
            rest_ref[...] = jnp.zeros_like(rest_ref)

    @pl.when(tower == 1)
    def _():
        cin_ref[...] = jnp.zeros_like(cin_ref)

    def finish(i, carry):
        peer = lax.rem(me + i, batch_count)
        value_copy(peer, me).wait_send()
        stat_copy(peer, me).wait_send()
        stat_copy(peer, peer).wait_recv()
        return carry

    lax.fori_loop(1, batch_count, finish, 0)
    stat_out_ref[...] = jnp.sum(stat_in_ref[...], axis=0)
    for c in range(columns):
        for q in range(TALL):
            out_ref[c : c + 1, q * BROAD : (q + 1) * BROAD] = total_ref[
                c * TALL + q : c * TALL + q + 1, :
            ]


def return_grads(
    grad_bags, codes, halves, served, stat, cins, rests, extras, windows, capacity, columns
):
    batch_count, rows_msg, _ = codes.shape
    micro_count = grad_bags.shape[0]
    slots = rows_msg * WIDE
    sizes = message_rows(rows_msg, columns)
    depth = batch_count // PLANE
    in_vmem = pl.BlockSpec(memory_space=pltpu.VMEM)
    dma = pltpu.SemaphoreType.DMA
    return pl.pallas_call(
        partial(return_kernel, capacity, micro_count, windows, columns),
        in_specs=[in_vmem] * 8,
        out_specs=[in_vmem] * 4,
        out_shape=[
            jax.ShapeDtypeStruct((columns, TALL * BROAD), jnp.float32),
            jax.ShapeDtypeStruct(stat.shape, jnp.float32),
            jax.ShapeDtypeStruct(cins.shape[1:], jnp.float32),
            jax.ShapeDtypeStruct(rests.shape[1:], jnp.float32),
        ],
        scratch_shapes=[
            pltpu.VMEM((batch_count, sizes, WIDE), jnp.bfloat16),
            pltpu.VMEM((batch_count, sizes, WIDE), jnp.bfloat16),
            pltpu.VMEM((sizes + 16, WIDE), jnp.float32),
            pltpu.VMEM((sizes + 16, WIDE), jnp.float32),
            pltpu.VMEM((columns * TALL, slots), jnp.bfloat16),
            pltpu.VMEM((BROAD, slots), jnp.bfloat16),
            pltpu.VMEM((columns * TALL, BROAD), jnp.float32),
            pltpu.VMEM((batch_count,) + stat.shape, jnp.float32),
            pltpu.VMEM(rests.shape, jnp.float32),
        ]
        + [
            pltpu.VMEM(lead + x.shape[1:], jnp.float32)
            for x in (cins, rests)
            for lead in ((PLANE, depth), (depth,), (depth,))
        ]
        + [dma((batch_count,))] * 10,
        compiler_params=pltpu.CompilerParams(
            vmem_limit_bytes=60 << 20, collective_id=1, has_side_effects=True
        ),
        name="return_grads",
    )(grad_bags, codes, halves, served, stat, cins, rests, extras)


def split_three(x):
    high = x.astype(jnp.bfloat16)
    rest = x - high.astype(jnp.float32)
    middle = rest.astype(jnp.bfloat16)
    low = (rest - middle.astype(jnp.float32)).astype(jnp.bfloat16)
    return high, middle, low


def dense_kernel(
    micro_count, windows, tower_ref, stat_ref, pooled_ref, label_ref, weight_ref,
    cins_ref, rests_ref, extras_ref,
    bags_ref, loss_ref, g_cins_ref, g_rests_ref, g_extras_ref,
    embed_ref, total_ref, pairs_ref, sym_ref, cin_ref, rest_ref, lane_ref,
):
    f32 = jnp.float32
    bf16 = jnp.bfloat16
    width = micro_count * LANES
    groups = HPAD // LANES

    cin_ref[...] = jnp.zeros_like(cin_ref)
    for b, at in enumerate(windows.cin_at):
        block = cins_ref[windows.slots[b]].astype(f32)
        cin_ref[at : at + windows.cin_rows, :] += block[: windows.cin_rows]
    rest_ref[...] = jnp.zeros_like(rest_ref)
    pieces = [(rests_ref, windows.slots[b], at) for b, at in enumerate(windows.rest_at)]
    pieces += [(extras_ref, e, at) for e, at in enumerate(windows.extra_at)]
    for source, b, at in pieces:
        skip = max(0, -at)
        block = source[b].astype(f32)
        for l in range(groups):
            rest_ref[l, at + skip : at + windows.rest_rows, :] += block[
                skip : windows.rest_rows, l * LANES : (l + 1) * LANES
            ]

    def rest_rows(begin, count):
        return jnp.concatenate(
            [rest_ref[l, begin : begin + count, :] for l in range(groups)], axis=1
        )[:, :HID]

    cin_w = cin_ref[:MAPS, :].astype(bf16)
    place = iota((MAPS, PAIRS), 0)
    place = place // FIELDS * FPAD + place % FIELDS == iota((MAPS, PAIRS), 1)
    picks_u = ones_at(place)
    row_u = jnp.broadcast_to(cin_ref[MAPS : MAPS + 1, :], (8, PAIRS)).astype(bf16)
    cin_u = dot(picks_u, row_u, NT)[:, :1]
    w_one = jnp.concatenate(
        [
            jnp.concatenate(
                [rest_ref[l, pl.ds(d, FPAD, stride=EMB), :] for l in range(groups)], axis=1
            )[:, :HID]
            for d in range(EMB)
        ],
        axis=0,
    ).astype(bf16)
    w_two = rest_rows(W_TWO, HID).astype(bf16)
    rows = jnp.zeros((8, HID), f32)
    for k, at in enumerate((B_ONE, B_TWO, W_THREE)):
        rows = jnp.where(iota((8, HID), 0) == k, rest_rows(at, 1), rows)
    unit = ones_at(iota((HID, HID), 0) == iota((HID, HID), 1))
    turned = dot(unit, rows.astype(bf16), NT)
    b_one, b_two, w_three = turned[:, 0:1], turned[:, 1:2], turned[:, 2:3]
    bias = rest_ref[0, BIAS : BIAS + 1, 0:1]

    def unpacked(row, count):
        pieces = []
        for m in range(micro_count):
            low = pooled_ref[m, row : row + HALF, :LANES]
            high = pooled_ref[m, row : row + HALF, LANES:]
            pieces.append(jnp.concatenate([low, high], axis=0)[:count])
        return jnp.concatenate(pieces, axis=1)

    for d in range(EMB):
        embed_ref[d * FPAD : (d + 1) * FPAD, :] = unpacked(d * HALF, FPAD)
    linear = jnp.concatenate(
        [
            pooled_ref[m, EMB * HALF : EMB * HALF + 1, :LANES]
            + pooled_ref[m, EMB * HALF : EMB * HALF + 1, LANES:]
            for m in range(micro_count)
        ],
        axis=1,
    )

    def pair_row(i, carry):
        total = jnp.zeros((FPAD, width), f32)
        for d in range(EMB):
            own = embed_ref[pl.ds(d * FPAD + i, 1), :]
            product = (embed_ref[d * FPAD : (d + 1) * FPAD, :] * own).astype(jnp.bfloat16)
            total = total + product.astype(f32)
        total_ref[pl.ds(pl.multiple_of(i * FPAD, 8), FPAD), :] = total
        return carry

    lax.fori_loop(0, FIELDS, pair_row, 0)
    thirds = split_three(total_ref[...])
    map_sum = sum(dot(cin_w, third) for third in thirds)
    cin_logits = jnp.sum(map_sum * cin_u, axis=0, keepdims=True)

    flat = embed_ref[...].astype(jnp.bfloat16)
    pre_one = dot(w_one, flat, TN) + b_one
    hidden_one = jnp.maximum(pre_one, 0.0).astype(jnp.bfloat16)
    pre_two = dot(w_two, hidden_one, TN) + b_two
    active_two = jnp.maximum(pre_two, 0.0)
    deep_logits = jnp.sum(active_two * w_three, axis=0, keepdims=True)
    logits = cin_logits + deep_logits + linear + bias

    samples = weight_ref.shape[1]
    lane_ref[...] = jnp.zeros_like(lane_ref)
    for m in range(micro_count):
        span = slice(m * LANES, m * LANES + samples)
        lane_ref[0:1, span] = weight_ref[m : m + 1, :].astype(f32)
        lane_ref[1:2, span] = label_ref[m : m + 1, :].astype(f32)
    weight = lane_ref[0:1, :]
    label = lane_ref[1:2, :]
    soft = jnp.maximum(logits, 0.0) + jnp.log1p(jnp.exp(-jnp.abs(logits)))
    loss_ref[...] = jnp.broadcast_to(
        jnp.sum(weight * (soft - label * logits), axis=1, keepdims=True), loss_ref.shape
    )
    grad_logits = weight * (jax.nn.sigmoid(logits) - label) / stat_ref[0:1, 0:1]

    grad_maps = (grad_logits * cin_u).astype(jnp.bfloat16)
    grad_two = jnp.where(pre_two > 0, grad_logits * w_three, 0.0).astype(jnp.bfloat16)
    grad_hidden = dot(w_two, grad_two)
    grad_one = jnp.where(pre_one > 0, grad_hidden, 0.0).astype(jnp.bfloat16)
    grad_flat = dot(w_one, grad_one)

    grad_pairs = dot(cin_w, grad_maps, TN)
    for m in range(micro_count):
        pairs_ref[m, :PAIRS, :] = grad_pairs[:, m * LANES : (m + 1) * LANES]
        pairs_ref[m, PAIRS:, :] = jnp.zeros((FPAD * FPAD - PAIRS, LANES), f32)

    def mirror(j, carry):
        here = pl.ds(pl.multiple_of(j * FPAD, 8), FPAD)
        both = [
            pairs_ref[m, here, :] + pairs_ref[m, pl.ds(j, FPAD, stride=FPAD), :]
            for m in range(micro_count)
        ]
        sym_ref[here, :] = jnp.concatenate(both, axis=1)
        return carry

    lax.fori_loop(0, FIELDS, mirror, 0)
    empty = jnp.zeros((2 * HALF - FPAD, width), f32)

    for d in range(EMB):

        def add_row(j, total):
            here = pl.ds(pl.multiple_of(j * FPAD, 8), FPAD)
            return total + sym_ref[here, :] * embed_ref[pl.ds(d * FPAD + j, 1), :]

        grad_embed = lax.fori_loop(
            0, FIELDS, add_row, grad_flat[d * FPAD : (d + 1) * FPAD], unroll=3
        )
        grad_embed = jnp.concatenate([grad_embed, empty], axis=0)
        for m in range(micro_count):
            span = slice(m * LANES, (m + 1) * LANES)
            block = jnp.concatenate([grad_embed[:HALF, span], grad_embed[HALF:, span]], axis=1)
            bags_ref[m, d * HALF : (d + 1) * HALF, :] = block.astype(bf16)
    for m in range(micro_count):
        row = grad_logits[:, m * LANES : (m + 1) * LANES]
        row = jnp.concatenate([row, row], axis=1)
        bags_ref[m, EMB * HALF :, :] = jnp.broadcast_to(row, (8, WIDE)).astype(bf16)

    ones = jnp.ones((8, width), bf16)

    def row_sum(x):
        return sum(dot(ones, third, NT) for third in split_three(x))[:1]

    rest_ref[...] = jnp.zeros_like(rest_ref)

    def put(begin, count, value, stride=None):
        for l in range(groups):
            piece = value[:, l * LANES : min((l + 1) * LANES, HID)]
            lanes = slice(0, piece.shape[1])
            if stride is None:
                rest_ref[l, begin : begin + count, lanes] = piece
            else:
                piece = jnp.pad(piece, ((0, 0), (0, LANES - piece.shape[1])))
                rest_ref[l, pl.ds(begin, count, stride=stride), :] = piece

    g_w_one = dot(flat, grad_one, NT)
    for d in range(EMB):
        put(d, FIELDS, g_w_one[d * FPAD : d * FPAD + FIELDS], EMB)

    @pl.when(tower_ref[0] == 0)
    def _():
        cin_ref[...] = jnp.zeros_like(cin_ref)
        cin_ref[:MAPS, :] = sum(dot(grad_maps, third, NT) for third in thirds)
        g_cin_u = jnp.sum(map_sum * grad_logits, axis=1, keepdims=True)
        thirds_u = split_three(jnp.broadcast_to(g_cin_u, (MAPS, 8)))
        cin_ref[MAPS : MAPS + 1, :] = sum(dot(third, picks_u, TN) for third in thirds_u)[:1]
        for b, at in enumerate(windows.cin_at):
            g_cins_ref[windows.slots[b], : windows.cin_rows, :] = cin_ref[
                at : at + windows.cin_rows, :
            ]
        for e, at in enumerate(windows.extra_at):
            skip = max(0, -at)
            for l in range(groups):
                span = slice(l * LANES, (l + 1) * LANES)
                g_extras_ref[e, skip : windows.rest_rows, span] = rest_ref[
                    l, at + skip : at + windows.rest_rows, :
                ]

    @pl.when(tower_ref[0] != 0)
    def _():
        put(W_TWO, HID, dot(hidden_one, grad_two, NT))
        put(B_ONE, 1, dot(ones, grad_one, NT)[:1])
        put(B_TWO, 1, dot(ones, grad_two, NT)[:1])
        put(W_THREE, 1, row_sum(active_two * grad_logits))
        g_bias = jnp.sum(grad_logits, axis=1, keepdims=True)
        put(BIAS, 1, jnp.where(iota((1, HID), 1) == 0, g_bias, 0.0))
        for b, at in enumerate(windows.rest_at):
            for l in range(groups):
                span = slice(l * LANES, (l + 1) * LANES)
                g_rests_ref[windows.slots[b], : windows.rest_rows, span] = rest_ref[
                    l, at : at + windows.rest_rows, :
                ]


def dense_step(tower_at, stats, pooled, labels, weights, cins, rests, extras, windows):
    micro_count = pooled.shape[0]
    width = micro_count * LANES
    in_vmem = pl.BlockSpec(memory_space=pltpu.VMEM)
    in_smem = pl.BlockSpec(memory_space=pltpu.SMEM)
    f32 = jnp.float32
    shapes = [
        ((micro_count, BAG_ROWS, WIDE), jnp.bfloat16),
        ((8, LANES), f32),
        (cins.shape, f32),
        (rests.shape, f32),
        (extras.shape, f32),
    ]
    return pl.pallas_call(
        partial(dense_kernel, micro_count, windows),
        in_specs=[in_smem] + [in_vmem] * 7,
        out_specs=[in_vmem] * len(shapes),
        out_shape=[jax.ShapeDtypeStruct(*shape) for shape in shapes],
        scratch_shapes=[
            pltpu.VMEM((EMB * FPAD, width), f32),
            pltpu.VMEM((PAIRS, width), f32),
            pltpu.VMEM((micro_count, FPAD * FPAD, LANES), f32),
            pltpu.VMEM((PAIRS, width), f32),
            pltpu.VMEM((windows.cin_total, PAIRS), f32),
            pltpu.VMEM((HPAD // LANES, windows.rest_total, LANES), f32),
            pltpu.VMEM((8, width), f32),
        ],
        compiler_params=pltpu.CompilerParams(vmem_limit_bytes=60 << 20),
        name="dense",
    )(tower_at.reshape(1), stats, pooled, labels, weights, cins, rests, extras)


def shards(
    shard_ids,
    local_rows,
    bag_counts,
    click_labels,
    sample_weights,
    embed_table,
    table_first,
    table_second,
    dense_params,
    dense_first,
    dense_second,
):
    tower_count = lax.axis_size("tower")
    batch_count = lax.axis_size("batch")
    tower_at = lax.axis_index("tower")
    micro_count, samples = shard_ids.shape[:2]
    columns, rows_dev = embed_table.shape
    capacity = 4 * samples * IDS_SAMP // (tower_count * batch_count)
    share = dense_params.shape[0]
    windows = Windows(share, batch_count)

    device = tower_at * batch_count + lax.axis_index("batch")
    cin_phase, rest_phase = windows.phases(device)
    low = dense_params.astype(jnp.bfloat16)

    def window(rows, row_size, phase):
        return lax.dynamic_update_slice(
            jnp.zeros((rows * row_size,), jnp.bfloat16), low, (phase,)
        )

    cin_window = window(windows.cin_rows, SQUARE, cin_phase).reshape(-1, FIELDS, FIELDS)
    cin_window = jnp.pad(
        cin_window,
        ((0, windows.cin_pad - windows.cin_rows), (0, 0), (0, FPAD - FIELDS)),
    ).reshape(windows.cin_pad, PAIRS)
    rest_window = jnp.pad(
        window(windows.rest_rows, HID, rest_phase).reshape(-1, HID),
        ((0, windows.rest_pad - windows.rest_rows), (0, HPAD - HID)),
    )

    def lanes_of(values):
        return jnp.moveaxis(values, 1, -1).reshape(micro_count, -1, samples)

    requests, codes, halves = route(
        lanes_of(shard_ids), lanes_of(local_rows), lanes_of(bag_counts), capacity, batch_count
    )
    pooled, served, stats, cins, rests, extras = fetch(
        requests, codes, halves, embed_table, sample_weights, cin_window, rest_window, windows,
        capacity, micro_count,
    )
    grad_bags, loss, g_cins, g_rests, g_extras = dense_step(
        tower_at, stats, pooled, click_labels, sample_weights, cins, rests, extras, windows
    )
    table_grad, losses, g_cin, g_rest = return_grads(
        grad_bags, codes, halves, served, loss, g_cins, g_rests, g_extras, windows, capacity, columns
    )
    g_cin = g_cin[: windows.cin_rows].reshape(-1, FIELDS, FPAD)[:, :, :FIELDS].reshape(-1)
    g_rest = g_rest[: windows.rest_rows, :HID].reshape(-1)
    is_cin = device * share + jnp.arange(share, dtype=jnp.int32) < CIN_SIZE
    own_grad = jnp.where(
        is_cin,
        lax.dynamic_slice(g_cin, (cin_phase,), (share,)),
        lax.dynamic_slice(g_rest, (rest_phase,), (share,)),
    )

    table_new, table_first_new, table_second_new = adam_update(
        embed_table, table_first, table_second, table_grad, rate_table
    )
    dense_new, dense_first_new, dense_second_new = adam_update(
        dense_params, dense_first, dense_second, own_grad, rate_dense
    )
    loss_sum = losses[0, 0] / stats[0, 0]
    return (
        table_new,
        table_first_new,
        table_second_new,
        table_new.astype(jnp.bfloat16),
        dense_new,
        dense_first_new,
        dense_second_new,
        dense_new.astype(jnp.bfloat16),
        loss_sum,
    )


def solution(mesh):
    rows = P(None, ("tower", "batch"))
    dense = P(("tower", "batch"))
    placed = (
        P(None, "batch", None, None),
        P(None, "batch", None, None),
        P(None, "batch", None),
        P(None, "batch"),
        P(None, "batch"),
        rows,
        rows,
        rows,
        dense,
        dense,
        dense,
    )
    return jax.shard_map(
        shards,
        mesh=mesh,
        in_specs=placed,
        out_specs=(rows, rows, rows, rows, dense, dense, dense, dense, P()),
        check_vma=False,
    )
```

profile of v0, /device:TPU:0, one launch (start us, length us, event | category | flops | bytes accessed | tf_op | source)
XLA Modules:
  0.0 209.2 jit_solution(4184784368451344379)
XLA Ops:
  0.6 30.7 %route.1 = (s32[16,13,256]{2,1,0:T(8,128)}, s32[16,13,256]{2,1,0:T(8,128)}, s32[16,13,256]{2,1,0:T(8,128)}) custom-call(s32[3,80,104]{2,1,0:T(8,128)} %bitcast.12, s32[3,80,104]{2,1,0:T(8,128)} %bitcast.13, s32[3,39,104]{2,1,0:T(8,128)} %bitcast.15), custom_call_target="tpu_custom_call" | custom-call | tf_op jit(solution)/shard_map/route/pallas_call | solution.py:219
  31.3 0.9 convert_element_type.13
  32.2 0.5 dynamic_update_slice.6
  32.8 0.2 reshape.49
  33.1 0.8 reshape.50.cin_ref
  33.8 0.5 dynamic_update_slice.7
  34.3 0.1 reshape.51
  34.5 0.6 pad.9.rest_ref
  35.1 74.4 %fetch.1 = (f32[3,248,256]{2,1,0:T(8,128)}, s32[16,13,256]{2,1,0:T(8,128)}, f32[8,128]{1,0:T(8,128)}, bf16[16,16,1560]{2,1,0:T(8,128)(2,1)}, bf16[16,64,512]{2,1,0:T(8,128)(2,1)}, /*index=5*/bf16[1,64,512]{2,1,0:T(8,128)(2,1)}) custom-call(s32[16,13,256]{2,1,0:T(8,128)} %get-tuple-element.27.req_ref, s32[16,13,256]{2,1,0:T(8,128)} %get-tuple-element.28.code_ref, ...), custom_call_target="tpu_custom_call" | custom-call | tf_op jit(solution)/shard_map/fetch/pallas_call | solution.py:559
  109.6 17.7 %dense.1 = (bf16[3,248,256]{2,1,0:T(8,128)(2,1)}, f32[8,128]{1,0:T(8,128)}, f32[16,16,1560]{2,1,0:T(8,128)}, f32[16,64,512]{2,1,0:T(8,128)}, f32[1,64,512]{2,1,0:T(8,128)}) custom-call(s32[1]{0:T(128)} %bitcast.tower_ref, f32[8,128]{1,0:T(8,128)} %get-tuple-element.30.stat_ref, f32[3,248,256]{2,1,0:T(8,128)} %get-tuple-element.31.pooled_ref, ...), custom_call_target="tpu_custom_call" | custom-call | tf_op jit(solution)/shard_map/dense/pallas_call | solution.py:1088
  127.3 0.0 copy-start
  127.3 68.6 %return_grads.1 = (f32[11,32768]{1,0:T(8,128)}, f32[8,128]{1,0:T(8,128)}, f32[16,1560]{1,0:T(8,128)}, f32[64,512]{1,0:T(8,128)}) custom-call(bf16[3,248,256]{2,1,0:T(8,128)(2,1)} %get-tuple-element.35.grad_ref, s32[16,13,256]{2,1,0:T(8,128)} %get-tuple-element.28.code_ref, s32[16,13,256]{2,1,0:T(8,128)} %get-tuple-element.29.half_ref, ...), custom_call_target="tpu_custom_call" | custom-call | tf_op jit(solution)/shard_map/return_grads/pallas_call | solution.py:825
  195.9 0.0 copy-done
  195.9 0.0 copy-start.3
  195.9 0.0 copy-start.2
  195.9 0.0 copy-start.1
  195.9 0.0 copy-start.4
  195.9 0.0 copy-start.5
  195.9 7.0 %fusion.4 = (bf16[11,32768]{1,0:T(8,128)(2,1)}, f32[11,32768]{1,0:T(8,128)}, f32[11,32768]{1,0:T(8,128)}, f32[11,32768]{1,0:T(8,128)}) fusion(f32[11,32768]{1,0:T(8,128)S(1)} %copy-done, f32[11,32768]{1,0:T(8,128)} %get-tuple-element.41, f32[11,32768]{1,0:T(8,128)} %param.17, f32[11,32768]{1,0:T(8,128)} %param.18), kind=kLoop, calls=%fused_computation.11 | loop fusion | flops 5767168 | bytes 10813440 | tf_op jit(solution)/shard_map/convert_element_type | solution.py:1184
  202.9 0.0 copy-done.3
  202.9 0.1 reshape.54
  203.1 0.0 copy-done.2
  203.1 0.2 reshape.52
  203.2 0.2 reshape.53
  203.5 0.0 copy-done.1
  203.5 0.0 copy-done.4
  203.5 0.0 copy-done.5
  203.5 0.8 fusion.2
  204.3 1.2 slice.18
  205.5 1.3 slice.19
  (4 shorter events, 0.1 us)
Async XLA Ops:
  127.3 68.6 %copy-start = (f32[11,32768]{1,0:T(8,128)S(1)}, f32[11,32768]{1,0:T(8,128)}, u32[]{:S(2)}) copy-start(f32[11,32768]{1,0:T(8,128)} %table_ref.1) | copy-start | bytes 4325380
  195.9 7.0 %copy-start.3 = (f32[64,512]{1,0:T(8,128)S(1)}, f32[64,512]{1,0:T(8,128)}, u32[]{:S(2)}) copy-start(f32[64,512]{1,0:T(8,128)} %get-tuple-element.43) | copy-start | bytes 393220
  195.9 7.2 %copy-start.2 = (f32[16,1560]{1,0:T(8,128)S(1)}, f32[16,1560]{1,0:T(8,128)}, u32[]{:S(2)}) copy-start(f32[16,1560]{1,0:T(8,128)} %get-tuple-element.42) | copy-start | bytes 299524
  195.9 7.6 %copy-start.1 = (f32[19426]{0:T(1024)S(1)}, f32[19426]{0:T(1024)}, u32[]{:S(2)}) copy-start(f32[19426]{0:T(1024)} %param.19) | copy-start | bytes 233116
  195.9 7.6 %copy-start.4 = (f32[19426]{0:T(1024)S(1)}, f32[19426]{0:T(1024)}, u32[]{:S(2)}) copy-start(f32[19426]{0:T(1024)} %param.20) | copy-start | bytes 233116
  195.9 7.6 %copy-start.5 = (f32[19426]{0:T(1024)S(1)}, f32[19426]{0:T(1024)}, u32[]{:S(2)}) copy-start(f32[19426]{0:T(1024)} %param.21) | copy-start | bytes 233116
where the time goes:
time: 212 us; the launch traced here: 209 us
  Pallas kernels  191 us (90%)
  other arithmetic  8.71 us (4%)
  local copies, waits for them, and re-layouts  5.83 us (3%)
  between operations  3.24 us (2%)
    pallas_call x1, Pallas kernels, fetch(): pl.pallas_call(partial(fetch_kernel, capacity, micro_count, windows, colu...  74.4 us
    pallas_call x1, Pallas kernels, return_grads(): pl.pallas_call(partial(return_kernel, capacity, micro_count, windows, col...  68.6 us
    pallas_call x1, Pallas kernels, route(): pl.pallas_call(partial(route_kernel, capacity, batch_count, micro_count),...  30.7 us
    pallas_call x1, Pallas kernels, dense_step(): pl.pallas_call(partial(dense_kernel, micro_count, windows), in_specs=[in_...  17.7 us
    convert_element_type x1, other arithmetic, shards(): table_new.astype(jnp.bfloat16)  6.98 us

commit v1 on v0

--- a/solution.py
+++ b/solution.py
@@ -55,6 +55,10 @@
     return lax.dot_general(a, b, dims, preferred_element_type=jnp.float32)
 
 
+def vmem_limit(batch_count):
+    return (28 + batch_count // 4) << 20
+
+
 def iota(shape, dim):
     return lax.broadcasted_iota(jnp.int32, shape, dim)
 
@@ -63,9 +67,9 @@
     return jnp.where(mask, 1.0, 0.0).astype(jnp.bfloat16)
 
 
-def layout_of(micro_count, capacity, size=WIDE):
-    first_rows = [m * capacity // size for m in range(micro_count)]
-    shifts = [m * capacity % size for m in range(micro_count)]
+def layout_of(micro_count, capacity):
+    first_rows = [m * capacity // WIDE for m in range(micro_count)]
+    shifts = [m * capacity % WIDE for m in range(micro_count)]
     window = max(-(-(shift + capacity) // WIDE) for shift in shifts)
     return first_rows, shifts, window, max(first_rows) + window
 
@@ -96,17 +100,12 @@
         return start % SQUARE, jnp.mod(start - CIN_SIZE, HID)
 
 
-def bf16_iota(rows, width):
-    return iota((rows, width), 0).astype(jnp.float32).astype(jnp.bfloat16)
-
-
 def route_kernel(
     capacity, batch_count, micro_count, ids_ref, rows_ref, counts_ref,
     req_ref, code_ref, half_ref, part_ref, left_ref, right_ref,
 ):
     f32, bf16 = jnp.float32, jnp.bfloat16
-    first_rows, shifts, window, _ = layout_of(micro_count, capacity, 2 * WIDE)
-    rows_msg = req_ref.shape[1]
+    first_rows, shifts, window, _ = layout_of(micro_count, capacity)
     micro = pl.program_id(0)
     id_rows, samples = ids_ref.shape[1:]
     chunk = 16
@@ -158,58 +157,52 @@
             )
     shift = sum(jnp.where(micro == m, shifts[m], 0) for m in range(micro_count))
     slot = rank.astype(jnp.int32) + shift
-    lane = slot % (2 * WIDE)
-    place = jnp.where(target < batch_count, (slot // (2 * WIDE)) * batch_count + target, -1)
+    place = jnp.where(target < batch_count, (slot // WIDE) * batch_count + target, -1)
     part_ref[0] = place.astype(f32)
-    part_ref[1] = jnp.where(lane < WIDE, lane, -1).astype(f32)
-    part_ref[2] = jnp.where(lane < WIDE, -1, lane - WIDE).astype(f32)
-    part_ref[3] = (local // WIDE).astype(f32)
-    part_ref[4] = (local % WIDE).astype(f32)
-    part_ref[5] = late * LANES + (iota((id_rows, LANES), 1) + 1).astype(f32)
-    part_ref[6] = field - late * HALF
+    part_ref[1] = (slot % WIDE).astype(f32)
+    part_ref[2] = (local // WIDE).astype(f32)
+    part_ref[3] = (local % WIDE).astype(f32)
+    part_ref[4] = late * LANES + (iota((id_rows, LANES), 1) + 1).astype(f32)
+    part_ref[5] = field - late * HALF
     places = window * batch_count
-    one, zero = jnp.ones((), bf16), jnp.zeros((), bf16)
 
     def build(t, carry):
         span = pl.ds(pl.multiple_of(t * LANES, LANES), LANES)
 
         def row(k):
-            return part_ref[k, pl.ds(t, 1), :].astype(bf16)
-
-        mask = bf16_iota(places, LANES) == row(0)
+            return part_ref[k, pl.ds(t, 1), :]
+
+        mask = iota((places, LANES), 0).astype(f32) == row(0)
         for v in range(4):
-            left_ref[v * places : (v + 1) * places, span] = jnp.where(mask, row(3 + v), zero)
-        for h in range(2):
-            right_ref[h * WIDE : (h + 1) * WIDE, span] = jnp.where(
-                bf16_iota(WIDE, LANES) == row(1 + h), one, zero
-            )
+            left_ref[v * places : (v + 1) * places, span] = jnp.where(
+                mask, row(2 + v), 0.0
+            ).astype(bf16)
+        right_ref[:, span] = ones_at(iota((WIDE, LANES), 0).astype(f32) == row(1))
         return carry
 
     lax.fori_loop(0, id_rows, build, 0, unroll=4)
     placed = dot(left_ref[...], right_ref[...], NT).astype(jnp.int32)
 
-    def part(v, r, h):
+    def part(v, r):
         begin = (v * window + r) * batch_count
-        return placed[begin : begin + batch_count, h * WIDE : (h + 1) * WIDE]
+        return placed[begin : begin + batch_count]
 
     for m in range(micro_count):
 
         @pl.when(micro == m)
         def _():
             for r in range(window):
-                for h in range(2):
-                    at = 2 * (first_rows[m] + r) + h
-                    if at < rows_msg:
-                        code = part(2, r, h)
-                        req_ref[:, at, :] += part(0, r, h) * WIDE + part(1, r, h)
-                        code_ref[:, at, :] += jnp.where(code > 0, code + m * WIDE, 0)
-                        half_ref[:, at, :] += part(3, r, h)
+                at = first_rows[m] + r
+                code = part(2, r)
+                req_ref[:, at, :] += part(0, r) * WIDE + part(1, r)
+                code_ref[:, at, :] += jnp.where(code > 0, code + m * WIDE, 0)
+                half_ref[:, at, :] += part(3, r)
 
 
 def route(ids, rows, counts, capacity, batch_count):
     micro_count, id_rows, samples = ids.shape
-    rows_msg = layout_of(micro_count, capacity)[3]
-    places = layout_of(micro_count, capacity, 2 * WIDE)[2] * batch_count
+    _, _, window, rows_msg = layout_of(micro_count, capacity)
+    places = window * batch_count
 
     def block(x):
         return pl.BlockSpec((1,) + x.shape[1:], lambda m: (m, 0, 0))
@@ -223,11 +216,11 @@
         out_specs=[whole] * 3,
         out_shape=[shape] * 3,
         scratch_shapes=[
-            pltpu.VMEM((7, id_rows, LANES), jnp.float32),
+            pltpu.VMEM((6, id_rows, LANES), jnp.float32),
             pltpu.VMEM((4 * places, id_rows * LANES), jnp.bfloat16),
-            pltpu.VMEM((2 * WIDE, id_rows * LANES), jnp.bfloat16),
+            pltpu.VMEM((WIDE, id_rows * LANES), jnp.bfloat16),
         ],
-        compiler_params=pltpu.CompilerParams(vmem_limit_bytes=60 << 20),
+        compiler_params=pltpu.CompilerParams(vmem_limit_bytes=vmem_limit(batch_count)),
         name="route",
     )(ids, rows, counts)
 
@@ -425,61 +418,6 @@
             span = slice(first_rows[m] * WIDE, (first_rows[m] + window) * WIDE)
             pooled_ref[m] += dot(left_ref[:, span], jnp.concatenate(rights, axis=1), NT)
 
-    pairs = batch_count // 2
-    lag = 2
-
-    def step(j, carry):
-        @pl.when(j < pairs)
-        def _():
-            first = lax.rem(me + batch_count - (2 * j + 1), batch_count)
-            second = lax.rem(me + 2 * batch_count - (2 * j + 2), batch_count)
-            request_copy(first, first).wait_recv()
-
-            @pl.when(j < pairs - 1)
-            def _():
-                request_copy(second, second).wait_recv()
-
-            look_up(first, second)
-
-            @pl.when(j == 0)
-            def _():
-                split(start_windows)
-
-            @pl.when((j == 0) & (tower == 0) & (me >= first_extra))
-            def _():
-                others(lambda peer: extra_copy(peer, me - first_extra).start())
-                extras_ref[me - first_extra] = rest_ref[...]
-
-            @pl.when(j == 3)
-            def _():
-                split(pass_windows)
-
-            answer_copy(first, me).start()
-
-            @pl.when(j < pairs - 1)
-            def _():
-                answer_copy(second, me).start()
-
-            @pl.when(j == pairs - 1)
-            def _():
-                own_copy().start()
-
-        @pl.when(j >= lag)
-        def _():
-            first = lax.rem(me + 2 * (j - lag) + 1, batch_count)
-            answer_copy(first, first).wait_recv()
-            pool(first)
-
-        @pl.when((j >= lag) & (j < pairs - 1 + lag))
-        def _():
-            second = lax.rem(me + 2 * (j - lag) + 2, batch_count)
-            answer_copy(second, second).wait_recv()
-            pool(second)
-
-        return carry
-
-    lax.fori_loop(0, pairs + lag, step, 0)
-
     def pair_copy(src, dst, k):
         return pltpu.make_async_remote_copy(
             src_ref=src,
@@ -490,22 +428,82 @@
             device_id_type=pl.DeviceIdType.MESH,
         )
 
-    @pl.when(tower == 0)
-    def _():
-        plane(lambda source: plane_copy(cins_ref, source, source).wait_recv())
-        for e in range(windows.extras):
-
-            @pl.when(me != first_extra + e)
+    def swap_windows():
+        @pl.when(tower == 0)
+        def _():
+            plane(lambda source: plane_copy(cins_ref, source, source).wait_recv())
+            for e in range(windows.extras):
+
+                @pl.when(me != first_extra + e)
+                def _():
+                    extra_copy(first_extra + e, e).wait_recv()
+
+            pair_copy(cins_ref, cins_ref, 0).start()
+            pair_copy(extras_ref, extras_ref, 1).start()
+
+        @pl.when(tower == 1)
+        def _():
+            plane(lambda source: plane_copy(rests_ref, source, source).wait_recv())
+            pair_copy(rests_ref, rests_ref, 0).start()
+
+    pairs = batch_count // 2
+    lag = 2
+
+    def step(j, carry):
+        @pl.when(j < pairs)
+        def _():
+            first = lax.rem(me + batch_count - (2 * j + 1), batch_count)
+            second = lax.rem(me + 2 * batch_count - (2 * j + 2), batch_count)
+            request_copy(first, first).wait_recv()
+
+            @pl.when(j < pairs - 1)
             def _():
-                extra_copy(first_extra + e, e).wait_recv()
-
-        pair_copy(cins_ref, cins_ref, 0).start()
-        pair_copy(extras_ref, extras_ref, 1).start()
-
-    @pl.when(tower == 1)
-    def _():
-        plane(lambda source: plane_copy(rests_ref, source, source).wait_recv())
-        pair_copy(rests_ref, rests_ref, 0).start()
+                request_copy(second, second).wait_recv()
+
+            look_up(first, second)
+
+            @pl.when(j == 0)
+            def _():
+                split(start_windows)
+
+            @pl.when((j == 0) & (tower == 0) & (me >= first_extra))
+            def _():
+                others(lambda peer: extra_copy(peer, me - first_extra).start())
+                extras_ref[me - first_extra] = rest_ref[...]
+
+            @pl.when(j == 3)
+            def _():
+                split(pass_windows)
+
+            @pl.when(j == pairs - 2)
+            def _():
+                swap_windows()
+
+            answer_copy(first, me).start()
+
+            @pl.when(j < pairs - 1)
+            def _():
+                answer_copy(second, me).start()
+
+            @pl.when(j == pairs - 1)
+            def _():
+                own_copy().start()
+
+        @pl.when(j >= lag)
+        def _():
+            first = lax.rem(me + 2 * (j - lag) + 1, batch_count)
+            answer_copy(first, first).wait_recv()
+            pool(first)
+
+        @pl.when((j >= lag) & (j < pairs - 1 + lag))
+        def _():
+            second = lax.rem(me + 2 * (j - lag) + 2, batch_count)
+            answer_copy(second, second).wait_recv()
+            pool(second)
+
+        return carry
+
+    lax.fori_loop(0, pairs + lag, step, 0)
 
     own_copy().wait()
     pool(me)
@@ -584,7 +582,7 @@
         + [dma((batch_count,))] * 11
         + [dma((windows.extras,)), dma((3,)), dma((3,))],
         compiler_params=pltpu.CompilerParams(
-            vmem_limit_bytes=60 << 20, collective_id=0, has_side_effects=True
+            vmem_limit_bytes=vmem_limit(batch_count), collective_id=0, has_side_effects=True
         ),
         name="fetch",
     )(requests, codes, halves, table, weights, cin_window, rest_window)
@@ -850,7 +848,7 @@
         ]
         + [dma((batch_count,))] * 10,
         compiler_params=pltpu.CompilerParams(
-            vmem_limit_bytes=60 << 20, collective_id=1, has_side_effects=True
+            vmem_limit_bytes=vmem_limit(batch_count), collective_id=1, has_side_effects=True
         ),
         name="return_grads",
     )(grad_bags, codes, halves, served, stat, cins, rests, extras)
@@ -947,7 +945,7 @@
         total_ref[pl.ds(pl.multiple_of(i * FPAD, 8), FPAD), :] = total
         return carry
 
-    lax.fori_loop(0, FIELDS, pair_row, 0)
+    lax.fori_loop(0, FIELDS, pair_row, 0, unroll=3)
     thirds = split_three(total_ref[...])
     map_sum = sum(dot(cin_w, third) for third in thirds)
     cin_logits = jnp.sum(map_sum * cin_u, axis=0, keepdims=True)
@@ -994,7 +992,7 @@
         sym_ref[here, :] = jnp.concatenate(both, axis=1)
         return carry
 
-    lax.fori_loop(0, FIELDS, mirror, 0)
+    lax.fori_loop(0, FIELDS, mirror, 0, unroll=3)
     empty = jnp.zeros((2 * HALF - FPAD, width), f32)
 
     for d in range(EMB):
@@ -1004,7 +1002,7 @@
             return total + sym_ref[here, :] * embed_ref[pl.ds(d * FPAD + j, 1), :]
 
         grad_embed = lax.fori_loop(
-            0, FIELDS, add_row, grad_flat[d * FPAD : (d + 1) * FPAD], unroll=3
+            0, FIELDS, add_row, grad_flat[d * FPAD : (d + 1) * FPAD], unroll=13
         )
         grad_embed = jnp.concatenate([grad_embed, empty], axis=0)
         for m in range(micro_count):
@@ -1099,7 +1097,7 @@
             pltpu.VMEM((HPAD // LANES, windows.rest_total, LANES), f32),
             pltpu.VMEM((8, width), f32),
         ],
-        compiler_params=pltpu.CompilerParams(vmem_limit_bytes=60 << 20),
+        compiler_params=pltpu.CompilerParams(vmem_limit_bytes=vmem_limit(windows.batch_count)),
         name="dense",
     )(tower_at.reshape(1), stats, pooled, labels, weights, cins, rests, extras)
 

time: 212 us -> 190 us (0.90)
  the two profiles are of different devices: /device:TPU:0 before, /device:TPU:30 now
where the time goes in v1:
time: 190 us
  Pallas kernels  173 us (91%)
  local copies, waits for them, and re-layouts  8.06 us (4%)
  other arithmetic  5.77 us (3%)
  between operations  3.27 us (2%)
    pallas_call x1, Pallas kernels, return_grads(): pl.pallas_call(partial(return_kernel, capacity, micro_count, windows, col...  73.5 us
    pallas_call x1, Pallas kernels, fetch(): pl.pallas_call(partial(fetch_kernel, capacity, micro_count, windows, colu...  65.4 us
    pallas_call x1, Pallas kernels, route(): pl.pallas_call(partial(route_kernel, capacity, batch_count, micro_count),...  20.8 us
    pallas_call x1, Pallas kernels, dense_step(): pl.pallas_call(partial(dense_kernel, micro_count, windows), in_specs=[in_...  12.8 us
    unnamed x24, local copies, waits for them, and re-layouts  4.93 us
    convert_element_type x1, other arithmetic, shards(): table_new.astype(jnp.bfloat16)  4.04 us

profile of v1, /device:TPU:30, one launch (start us, length us, event | category | flops | bytes accessed | tf_op | source)
XLA Modules:
  0.0 189.6 jit_solution(4821835993509170276)
XLA Ops:
  0.7 0.9 copy-done.2
  1.6 0.9 copy-done.3
  2.5 0.8 copy-done.4
  3.3 20.8 %route.1 = (s32[16,13,256]{2,1,0:T(8,128)S(1)}, s32[16,13,256]{2,1,0:T(8,128)S(1)}, s32[16,13,256]{2,1,0:T(8,128)S(1)}) custom-call(s32[3,80,104]{2,1,0:T(8,128)S(1)} %bitcast.11, s32[3,80,104]{2,1,0:T(8,128)S(1)} %bitcast.12, s32[3,39,104]{2,1,0:T(8,128)S(1)} %bitcast.14), custom_call_target="tpu_custom_call" | custom-call | tf_op jit(solution)/shard_map/route/pallas_call | solution.py:212
  24.1 0.9 convert_element_type.13
  25.0 0.5 dynamic_update_slice.6
  25.5 0.2 reshape.49
  25.8 0.1 reshape.50.cin_ref
  26.0 0.5 dynamic_update_slice.7
  26.5 0.1 reshape.51
  26.7 0.0 copy-start
  26.7 1.6 copy-done
  28.3 0.7 copy-done.5
  29.0 65.4 %fetch.1 = (f32[3,248,256]{2,1,0:T(8,128)S(1)}, s32[16,13,256]{2,1,0:T(8,128)S(1)}, f32[8,128]{1,0:T(8,128)S(1)}, bf16[16,16,1560]{2,1,0:T(8,128)(2,1)S(1)}, bf1...) custom-call(s32[16,13,256]{2,1,0:T(8,128)S(1)} %get-tuple-element.27.req_ref, ...), custom_call_target="tpu_custom_call" | custom-call | tf_op jit(solution)/shard_map/fetch/pallas_call | solution.py:557
  94.4 0.0 copy-start.8
  94.4 12.8 %dense.1 = (bf16[3,248,256]{2,1,0:T(8,128)(2,1)S(1)}, f32[8,128]{1,0:T(8,128)S(1)}, f32[16,16,1560]{2,1,0:T(8,128)S(1)}, f32[16,64,512]{2,1,0:T(8,128)S(1)}, f32[1,64,512]{2,1,0:T(8,128)S(1)}) custom-call(s32[1]{0:T(128)} %bitcast.tower_ref, f32[8,128]{1,0:T(8,128)S(1)} %get-tuple-element.30.stat_ref, f32[3,248,256]{2,1,0:T(8,128)S(1)} %get-tuple-element.31.pooled_ref, ...), custom_call_target="tpu_custom_call" | custom-call | tf_op jit(solution)/shard_map/dense/pallas_call | solution.py:1086
  107.2 0.0 copy-start.1
  107.2 0.0 copy-start.7
  107.3 73.5 %return_grads.1 = (f32[11,32768]{1,0:T(8,128)S(1)}, f32[8,128]{1,0:T(8,128)S(1)}, f32[16,1560]{1,0:T(8,128)S(1)}, f32[64,512]{1,0:T(8,128)S(1)}) custom-call(bf16[3,248,256]{2,1,0:T(8,128)(2,1)S(1)} %get-tuple-element.35.grad_ref, s32[16,13,256]{2,1,0:T(8,128)S(1)} %get-tuple-element.28.code_ref, s32[16,13,256]{2,1,0:T(8,128)S(1)} %get-tuple-element.29.half_ref, ...), custom_call_target="tpu_custom_call" | custom-call | tf_op jit(solution)/shard_map/return_grads/pallas_call | solution.py:823
  180.8 0.0 copy-done.8
  180.8 0.0 copy-done.1
  180.8 0.0 copy-done.7
  180.8 0.0 copy-start.9
  180.8 0.0 copy-start.10
  180.9 0.0 copy-start.11
  180.9 4.0 %fusion.4 = (bf16[11,32768]{1,0:T(8,128)(2,1)}, f32[11,32768]{1,0:T(8,128)}, f32[11,32768]{1,0:T(8,128)}, f32[11,32768]{1,0:T(8,128)}) fusion(f32[11,32768]{1,0:T(8,128)S(1)} %copy-done.1, f32[11,32768]{1,0:T(8,128)S(1)} %get-tuple-element.41, f32[11,32768]{1,0:T(8,128)S(1)} %copy-done.7, f32[11,32768]{1,0:T(8,128)S(1)} %copy-done.8), kind=kLoop, calls=%fused_computation.11 | loop fusion | flops 5767168 | bytes 10813440 | tf_op jit(solution)/shard_map/convert_element_type | solution.py:1182
  184.9 0.1 reshape.54
  185.0 0.2 reshape.52
  185.2 0.2 reshape.53
  185.5 0.8 fusion.2
  186.3 0.5 slice.18
  186.8 0.5 slice.19
  (14 shorter events, 0.1 us)
Async XLA Ops:
  0.6 0.9 copy-start.2
  1.6 0.9 copy-start.3
  2.5 0.8 copy-start.4
  25.0 69.4 %copy-start.6 = (s32[3,104]{1,0:T(4,128)S(1)}, s32[3,104]{1,0:T(4,128)}, u32[]{:S(2)}) copy-start(s32[3,104]{1,0:T(4,128)} %label_ref.1) | copy-start | bytes 3748
  26.7 1.6 copy-start
  28.3 0.7 copy-start.5
  94.4 86.4 %copy-start.8 = (f32[11,32768]{1,0:T(8,128)S(1)}, f32[11,32768]{1,0:T(8,128)}, u32[]{:S(2)}) copy-start(f32[11,32768]{1,0:T(8,128)} %param.18) | copy-start | bytes 4325380
  107.2 73.6 %copy-start.1 = (f32[11,32768]{1,0:T(8,128)S(1)}, f32[11,32768]{1,0:T(8,128)}, u32[]{:S(2)}) copy-start(f32[11,32768]{1,0:T(8,128)} %table_ref.1) | copy-start | bytes 4325380
  107.2 73.6 %copy-start.7 = (f32[11,32768]{1,0:T(8,128)S(1)}, f32[11,32768]{1,0:T(8,128)}, u32[]{:S(2)}) copy-start(f32[11,32768]{1,0:T(8,128)} %param.17) | copy-start | bytes 4325380
  180.8 4.6 %copy-start.9 = (f32[19426]{0:T(1024)S(1)}, f32[19426]{0:T(1024)}, u32[]{:S(2)}) copy-start(f32[19426]{0:T(1024)} %param.19) | copy-start | bytes 233116
  180.8 4.6 %copy-start.10 = (f32[19426]{0:T(1024)S(1)}, f32[19426]{0:T(1024)}, u32[]{:S(2)}) copy-start(f32[19426]{0:T(1024)} %param.20) | copy-start | bytes 233116
  180.9 4.6 %copy-start.11 = (f32[19426]{0:T(1024)S(1)}, f32[19426]{0:T(1024)}, u32[]{:S(2)}) copy-start(f32[19426]{0:T(1024)} %param.21) | copy-start | bytes 233116

commit v2 on v1

--- a/solution.py
+++ b/solution.py
@@ -67,11 +67,24 @@
     return jnp.where(mask, 1.0, 0.0).astype(jnp.bfloat16)
 
 
-def layout_of(micro_count, capacity):
-    first_rows = [m * capacity // WIDE for m in range(micro_count)]
-    shifts = [m * capacity % WIDE for m in range(micro_count)]
-    window = max(-(-(shift + capacity) // WIDE) for shift in shifts)
-    return first_rows, shifts, window, max(first_rows) + window
+class Slots:
+    def __init__(self, micro_count, capacity):
+        self.micro_count = micro_count
+        self.first_rows = [m * capacity // WIDE for m in range(micro_count)]
+        self.shifts = [m * capacity % WIDE for m in range(micro_count)]
+        self.spans = [-(-(shift + capacity) // LANES) * LANES for shift in self.shifts]
+        self.length = max(
+            first * WIDE + span for first, span in zip(self.first_rows, self.spans)
+        )
+        self.rows = -(-self.length // WIDE)
+        self.window = max(-(-span // WIDE) for span in self.spans)
+
+    def width(self, row):
+        return min(WIDE, self.length - row * WIDE)
+
+    def micro_width(self, micro, row):
+        inside = row - self.first_rows[micro]
+        return max(0, min(WIDE, self.spans[micro] - inside * WIDE)) if inside >= 0 else 0
 
 
 class Windows:
@@ -81,6 +94,8 @@
         self.rest_rows = -(-(HID - 1 + share) // HID)
         self.cin_pad = -(-self.cin_rows // 16) * 16
         self.rest_pad = -(-self.rest_rows // 16) * 16
+        self.cin_pad_wide = -(-self.cin_rows // 8) * 8
+        self.rest_pad_wide = -(-self.rest_rows // 8) * 8
         self.first_extra = CIN_SIZE // share
         self.extras = batch_count - self.first_extra
         self.cin_at = [b * share // SQUARE for b in range(batch_count)]
@@ -101,11 +116,11 @@
 
 
 def route_kernel(
-    capacity, batch_count, micro_count, ids_ref, rows_ref, counts_ref,
+    slots, batch_count, ids_ref, rows_ref, counts_ref,
     req_ref, code_ref, half_ref, part_ref, left_ref, right_ref,
 ):
     f32, bf16 = jnp.float32, jnp.bfloat16
-    first_rows, shifts, window, _ = layout_of(micro_count, capacity)
+    micro_count, window = slots.micro_count, slots.window
     micro = pl.program_id(0)
     id_rows, samples = ids_ref.shape[1:]
     chunk = 16
@@ -155,7 +170,7 @@
             rank = rank + jnp.where(
                 target == begin + d, ranks[d * id_rows : (d + 1) * id_rows], 0.0
             )
-    shift = sum(jnp.where(micro == m, shifts[m], 0) for m in range(micro_count))
+    shift = sum(jnp.where(micro == m, slots.shifts[m], 0) for m in range(micro_count))
     slot = rank.astype(jnp.int32) + shift
     place = jnp.where(target < batch_count, (slot // WIDE) * batch_count + target, -1)
     part_ref[0] = place.astype(f32)
@@ -192,25 +207,30 @@
         @pl.when(micro == m)
         def _():
             for r in range(window):
-                at = first_rows[m] + r
+                at = slots.first_rows[m] + r
+                if slots.micro_width(m, at) == 0:
+                    continue
                 code = part(2, r)
                 req_ref[:, at, :] += part(0, r) * WIDE + part(1, r)
                 code_ref[:, at, :] += jnp.where(code > 0, code + m * WIDE, 0)
                 half_ref[:, at, :] += part(3, r)
 
 
-def route(ids, rows, counts, capacity, batch_count):
+def in_hbm(x):
+    return pltpu.with_memory_space_constraint(x, pltpu.HBM)
+
+
+def route(ids, rows, counts, slots, batch_count):
     micro_count, id_rows, samples = ids.shape
-    _, _, window, rows_msg = layout_of(micro_count, capacity)
-    places = window * batch_count
+    places = slots.window * batch_count
 
     def block(x):
         return pl.BlockSpec((1,) + x.shape[1:], lambda m: (m, 0, 0))
 
-    whole = pl.BlockSpec((batch_count, rows_msg, WIDE), lambda m: (0, 0, 0))
-    shape = jax.ShapeDtypeStruct((batch_count, rows_msg, WIDE), jnp.int32)
+    whole = pl.BlockSpec((batch_count, slots.rows, WIDE), lambda m: (0, 0, 0))
+    shape = jax.ShapeDtypeStruct((batch_count, slots.rows, WIDE), jnp.int32)
     return pl.pallas_call(
-        partial(route_kernel, capacity, batch_count, micro_count),
+        partial(route_kernel, slots, batch_count),
         grid=(micro_count,),
         in_specs=[block(ids), block(rows), block(counts)],
         out_specs=[whole] * 3,
@@ -222,7 +242,7 @@
         ],
         compiler_params=pltpu.CompilerParams(vmem_limit_bytes=vmem_limit(batch_count)),
         name="route",
-    )(ids, rows, counts)
+    )(in_hbm(ids), in_hbm(rows), in_hbm(counts))
 
 
 def peer_copy(src, dst, send_sem, recv_sem, peer):
@@ -256,7 +276,10 @@
             device_id={"tower": other_tower},
             device_id_type=pl.DeviceIdType.MESH,
         )
-    pl.semaphore_wait(barrier, batch_count - (1 if other_tower is None else 0))
+
+
+def all_greeted(batch_count, pair):
+    pl.semaphore_wait(pltpu.get_barrier_semaphore(), batch_count - 1 + (1 if pair else 0))
 
 
 def message_rows(rows_msg, columns):
@@ -290,21 +313,26 @@
 
 
 def fetch_kernel(
-    capacity, micro_count, windows, columns,
-    req_ref, code_ref, half_ref, table_ref, weight_ref, cin_ref, rest_ref,
+    slots, windows, columns,
+    req_ref, code_ref, half_ref, table_hbm_ref, weight_ref, cin_ref, rest_ref,
     out_ref, served_ref, stat_out_ref, cins_ref, rests_ref, extras_ref,
-    tiles_ref, stage_ref, first_ref, second_ref, ans_out_ref, ans_in_ref, left_ref, pooled_ref,
+    table_ref, tiles_ref, stage_ref, first_ref, second_ref, ans_out_ref, ans_in_ref, left_ref, pooled_ref,
     other_ref, stat_ref, stat_in_ref,
     req_send, req_recv, ans_send, ans_recv, stat_send, stat_recv, win_send, win_recv, plane_send,
-    plane_recv, ext_send, ext_recv, pair_send, pair_recv,
+    plane_recv, ext_send, ext_recv, pair_send, pair_recv, table_sem,
 ):
-    first_rows, _, window, rows_msg = layout_of(micro_count, capacity)
+    rows_msg = slots.rows
     batch_count = windows.batch_count
     first_extra = windows.first_extra
     me = lax.axis_index("batch")
     tower = lax.axis_index("tower")
     other_tower = 1 - tower
     greet(me, batch_count, other_tower)
+    load_table = pltpu.make_async_copy(table_hbm_ref, table_ref, table_sem)
+    load_table.start()
+    pooled_ref[...] = jnp.zeros_like(pooled_ref)
+    first_ref[...] = jnp.zeros_like(first_ref)
+    second_ref[...] = jnp.zeros_like(second_ref)
 
     def request_copy(peer, slot):
         return peer_copy(
@@ -323,6 +351,8 @@
 
     def own_copy():
         return pltpu.make_async_copy(ans_out_ref.at[me], ans_in_ref.at[me], ans_recv.at[me])
+
+    all_greeted(batch_count, True)
 
     def send_requests(i, carry):
         peer = lax.rem(me + i, batch_count)
@@ -382,41 +412,49 @@
 
     served_ref[me] = req_ref[me]
     stat_in_ref[me] = stat_ref[...]
+    load_table.wait()
     tile_table(table_ref, tiles_ref, stage_ref, columns)
-    pooled_ref[...] = jnp.zeros_like(pooled_ref)
 
     sizes = ans_out_ref.shape[1]
 
     def look_up(first, second):
         for r in range(rows_msg):
+            w = slots.width(r)
             row = jnp.concatenate(
-                [served_ref[first, r : r + 1, :], served_ref[second, r : r + 1, :]], axis=1
+                [served_ref[first, r : r + 1, :w], served_ref[second, r : r + 1, :w]], axis=1
             )
-            hot = ones_at(iota((BROAD, 2 * WIDE), 0) == row % BROAD)
+            hot = ones_at(iota((BROAD, 2 * w), 0) == row % BROAD)
             result = dot(tiles_ref[...], hot)
-            mask = iota((TALL, 2 * WIDE), 0) == row // BROAD
+            mask = iota((TALL, 2 * w), 0) == row // BROAD
             block = pick_rows(result, mask, TALL, columns)
-            first_ref[r * columns : r * columns + 16, :] = block[:, :WIDE]
-            second_ref[r * columns : r * columns + 16, :] = block[:, WIDE:]
+            first_ref[r * columns : r * columns + 16, :w] = block[:, :w]
+            second_ref[r * columns : r * columns + 16, :w] = block[:, w:]
         ans_out_ref[first] = first_ref[:sizes, :].astype(jnp.bfloat16)
         ans_out_ref[second] = second_ref[:sizes, :].astype(jnp.bfloat16)
 
     def pool(owner):
         first_ref[:sizes, :] = ans_in_ref[owner].astype(jnp.float32)
         for r in range(rows_msg):
-            span = slice(r * WIDE, (r + 1) * WIDE)
-            values = [first_ref[r * columns + c : r * columns + c + 1, :] for c in range(columns)]
-            mask = iota((HALF, WIDE), 0) == half_ref[owner, r : r + 1, :]
+            w = slots.width(r)
+            begin = r * columns
+            values = [first_ref[begin + c : begin + c + 1, :w] for c in range(columns)]
+            mask = iota((HALF, w), 0) == half_ref[owner, r : r + 1, :w]
             pieces = [jnp.where(mask, values[c], 0.0) for c in range(EMB)]
-            pieces.append(jnp.where(iota((8, WIDE), 0) == 0, values[EMB], 0.0))
-            left_ref[:, span] = jnp.concatenate(pieces, axis=0).astype(jnp.bfloat16)
-        for m in range(micro_count):
-            rights = [
-                ones_at(iota((WIDE, WIDE), 0) + (m * WIDE + 1) == code_ref[owner, r : r + 1, :])
-                for r in range(first_rows[m], first_rows[m] + window)
-            ]
-            span = slice(first_rows[m] * WIDE, (first_rows[m] + window) * WIDE)
-            pooled_ref[m] += dot(left_ref[:, span], jnp.concatenate(rights, axis=1), NT)
+            pieces.append(jnp.where(iota((8, w), 0) == 0, values[EMB], 0.0))
+            left_ref[:, r * WIDE : r * WIDE + w] = jnp.concatenate(pieces, axis=0).astype(
+                jnp.bfloat16
+            )
+        for m in range(slots.micro_count):
+            rights = []
+            for r in range(slots.first_rows[m], rows_msg):
+                w = slots.micro_width(m, r)
+                if w:
+                    lane = iota((WIDE, w), 0) + (m * WIDE + 1)
+                    rights.append(ones_at(lane == code_ref[owner, r : r + 1, :w]))
+            begin = slots.first_rows[m] * WIDE
+            pooled_ref[m] += dot(
+                left_ref[:, begin : begin + slots.spans[m]], jnp.concatenate(rights, axis=1), NT
+            )
 
     def pair_copy(src, dst, k):
         return pltpu.make_async_remote_copy(
@@ -545,18 +583,17 @@
 
 
 def fetch(
-    requests, codes, halves, table, weights, cin_window, rest_window, windows, capacity, micro_count
+    requests, codes, halves, table, weights, cin_window, rest_window, windows, slots
 ):
     batch_count, rows_msg, _ = requests.shape
     columns, rows_dev = table.shape
-    slots = rows_msg * WIDE
     sizes = message_rows(rows_msg, columns)
     in_vmem = pl.BlockSpec(memory_space=pltpu.VMEM)
     dma = pltpu.SemaphoreType.DMA
-    bags = (micro_count, BAG_ROWS, WIDE)
+    bags = (slots.micro_count, BAG_ROWS, WIDE)
     return pl.pallas_call(
-        partial(fetch_kernel, capacity, micro_count, windows, columns),
-        in_specs=[in_vmem] * 7,
+        partial(fetch_kernel, slots, windows, columns),
+        in_specs=[in_vmem] * 3 + [pl.BlockSpec(memory_space=pltpu.HBM)] + [in_vmem] * 3,
         out_specs=[in_vmem] * 6,
         out_shape=[
             jax.ShapeDtypeStruct(bags, jnp.float32),
@@ -567,29 +604,30 @@
             jax.ShapeDtypeStruct((windows.extras,) + rest_window.shape, jnp.bfloat16),
         ],
         scratch_shapes=[
+            pltpu.VMEM(table.shape, jnp.float32),
             pltpu.VMEM((columns * TALL, BROAD), jnp.bfloat16),
             pltpu.VMEM((TALL, BROAD), jnp.float32),
             pltpu.VMEM((sizes + 16, WIDE), jnp.float32),
             pltpu.VMEM((sizes + 16, WIDE), jnp.float32),
             pltpu.VMEM((batch_count, sizes, WIDE), jnp.bfloat16),
             pltpu.VMEM((batch_count, sizes, WIDE), jnp.bfloat16),
-            pltpu.VMEM((BAG_ROWS, slots), jnp.bfloat16),
+            pltpu.VMEM((BAG_ROWS, rows_msg * WIDE), jnp.bfloat16),
             pltpu.VMEM(bags, jnp.float32),
             pltpu.VMEM(bags, jnp.float32),
             pltpu.VMEM((8, LANES), jnp.float32),
             pltpu.VMEM((batch_count, 8, LANES), jnp.float32),
         ]
         + [dma((batch_count,))] * 11
-        + [dma((windows.extras,)), dma((3,)), dma((3,))],
+        + [dma((windows.extras,)), dma((3,)), dma((3,)), dma],
         compiler_params=pltpu.CompilerParams(
             vmem_limit_bytes=vmem_limit(batch_count), collective_id=0, has_side_effects=True
         ),
         name="fetch",
-    )(requests, codes, halves, table, weights, cin_window, rest_window)
+    )(requests, codes, halves, in_hbm(table), weights, cin_window, rest_window)
 
 
 def return_kernel(
-    capacity, micro_count, windows, columns,
+    slots, windows, columns,
     grad_ref, code_ref, half_ref, served_ref, stat_ref, cins_ref, rests_ref, extras_ref,
     out_ref, stat_out_ref, cin_ref, rest_ref,
     send_ref, recv_ref, first_ref, second_ref, left_ref, right_ref, total_ref, stat_in_ref,
@@ -600,7 +638,7 @@
     batch_count = windows.batch_count
     first_extra = windows.first_extra
     tower = lax.axis_index("tower")
-    first_rows, _, window, rows_msg = layout_of(micro_count, capacity)
+    rows_msg = slots.rows
     me = lax.axis_index("batch")
     greet(me, batch_count)
 
@@ -676,46 +714,56 @@
         stat_copy(lax.rem(me + i, batch_count), me).start()
         return carry
 
-    lax.fori_loop(1, batch_count, send_stats, 0)
+    first_ref[...] = jnp.zeros_like(first_ref)
+    second_ref[...] = jnp.zeros_like(second_ref)
     stat_in_ref[me] = stat_ref[...]
     total_ref[...] = jnp.zeros_like(total_ref)
 
     sizes = send_ref.shape[1]
 
     def spread(first, second):
+        def both(ref, r, w):
+            return jnp.concatenate([ref[first, r : r + 1, :w], ref[second, r : r + 1, :w]], axis=1)
+
         for r in range(rows_msg):
-            code = jnp.concatenate(
-                [code_ref[first, r : r + 1, :], code_ref[second, r : r + 1, :]], axis=1
-            )
-            half = jnp.concatenate(
-                [half_ref[first, r : r + 1, :], half_ref[second, r : r + 1, :]], axis=1
-            )
+            w = slots.width(r)
             result = None
-            for m in range(micro_count):
-                if first_rows[m] <= r < first_rows[m] + window:
-                    hot = ones_at(iota((WIDE, 2 * WIDE), 0) + (m * WIDE + 1) == code)
-                    found = dot(grad_ref[m], hot)
-                    result = found if result is None else result + found
-            block = pick_rows(result, iota((HALF, 2 * WIDE), 0) == half, HALF, EMB)
+            for m in range(slots.micro_count):
+                inner = slots.micro_width(m, r)
+                if inner == 0:
+                    continue
+                hot = ones_at(iota((WIDE, 2 * inner), 0) + (m * WIDE + 1) == both(code_ref, r, inner))
+                found = dot(grad_ref[m], hot)
+                if inner < w:
+                    blank = jnp.zeros((BAG_ROWS, w - inner), jnp.float32)
+                    found = jnp.concatenate(
+                        [found[:, :inner], blank, found[:, inner:], blank], axis=1
+                    )
+                result = found if result is None else result + found
+            mask = iota((HALF, 2 * w), 0) == both(half_ref, r, w)
+            block = pick_rows(result, mask, HALF, EMB)
             linear = result[EMB * HALF : EMB * HALF + 1]
-            block = jnp.where(iota((16, 2 * WIDE), 0) == EMB, linear, block)
-            first_ref[r * columns : r * columns + 16, :] = block[:, :WIDE]
-            second_ref[r * columns : r * columns + 16, :] = block[:, WIDE:]
+            block = jnp.where(iota((16, 2 * w), 0) == EMB, linear, block)
+            first_ref[r * columns : r * columns + 16, :w] = block[:, :w]
+            second_ref[r * columns : r * columns + 16, :w] = block[:, w:]
         send_ref[first] = first_ref[:sizes, :].astype(jnp.bfloat16)
         send_ref[second] = second_ref[:sizes, :].astype(jnp.bfloat16)
 
     def scatter(source):
         first_ref[:sizes, :] = recv_ref[source].astype(jnp.float32)
         for r in range(rows_msg):
-            span = slice(r * WIDE, (r + 1) * WIDE)
-            row = served_ref[source, r : r + 1, :]
-            mask = iota((TALL, WIDE), 0) == row // BROAD
+            w = slots.width(r)
+            span = slice(r * WIDE, r * WIDE + w)
+            row = served_ref[source, r : r + 1, :w]
+            mask = iota((TALL, w), 0) == row // BROAD
             for c in range(columns):
                 left_ref[c * TALL : (c + 1) * TALL, span] = jnp.where(
-                    mask, first_ref[r * columns + c : r * columns + c + 1, :], 0.0
+                    mask, first_ref[r * columns + c : r * columns + c + 1, :w], 0.0
                 ).astype(jnp.bfloat16)
-            right_ref[:, span] = ones_at(iota((BROAD, WIDE), 0) == row % BROAD)
-        total_ref[...] += dot(left_ref[...], right_ref[...], NT)
+            right_ref[:, span] = ones_at(iota((BROAD, w), 0) == row % BROAD)
+        total_ref[...] += dot(
+            left_ref[:, : slots.length], right_ref[:, : slots.length], NT
+        )
 
     pairs = batch_count // 2
     lag = 2
@@ -726,6 +774,12 @@
             first = lax.rem(me + 2 * j + 1, batch_count)
             second = lax.rem(me + 2 * j + 2, batch_count)
             spread(first, second)
+
+            @pl.when(j == 0)
+            def _():
+                all_greeted(batch_count, False)
+                lax.fori_loop(1, batch_count, send_stats, 0)
+
             value_copy(first, me).start()
 
             @pl.when(j == 1)
@@ -811,17 +865,16 @@
 
 
 def return_grads(
-    grad_bags, codes, halves, served, stat, cins, rests, extras, windows, capacity, columns
+    grad_bags, codes, halves, served, stat, cins, rests, extras, windows, slots, columns
 ):
     batch_count, rows_msg, _ = codes.shape
-    micro_count = grad_bags.shape[0]
-    slots = rows_msg * WIDE
+    long = rows_msg * WIDE
     sizes = message_rows(rows_msg, columns)
     depth = batch_count // PLANE
     in_vmem = pl.BlockSpec(memory_space=pltpu.VMEM)
     dma = pltpu.SemaphoreType.DMA
     return pl.pallas_call(
-        partial(return_kernel, capacity, micro_count, windows, columns),
+        partial(return_kernel, slots, windows, columns),
         in_specs=[in_vmem] * 8,
         out_specs=[in_vmem] * 4,
         out_shape=[
@@ -835,8 +888,8 @@
             pltpu.VMEM((batch_count, sizes, WIDE), jnp.bfloat16),
             pltpu.VMEM((sizes + 16, WIDE), jnp.float32),
             pltpu.VMEM((sizes + 16, WIDE), jnp.float32),
-            pltpu.VMEM((columns * TALL, slots), jnp.bfloat16),
-            pltpu.VMEM((BROAD, slots), jnp.bfloat16),
+            pltpu.VMEM((columns * TALL, long), jnp.bfloat16),
+            pltpu.VMEM((BROAD, long), jnp.bfloat16),
             pltpu.VMEM((columns * TALL, BROAD), jnp.float32),
             pltpu.VMEM((batch_count,) + stat.shape, jnp.float32),
             pltpu.VMEM(rests.shape, jnp.float32),
@@ -1079,9 +1132,9 @@
     shapes = [
         ((micro_count, BAG_ROWS, WIDE), jnp.bfloat16),
         ((8, LANES), f32),
-        (cins.shape, f32),
-        (rests.shape, f32),
-        (extras.shape, f32),
+        ((cins.shape[0], windows.cin_pad_wide, PAIRS), f32),
+        ((rests.shape[0], windows.rest_pad_wide, HPAD), f32),
+        ((extras.shape[0], windows.rest_pad_wide, HPAD), f32),
     ]
     return pl.pallas_call(
         partial(dense_kernel, micro_count, windows),
@@ -1123,6 +1176,7 @@
     capacity = 4 * samples * IDS_SAMP // (tower_count * batch_count)
     share = dense_params.shape[0]
     windows = Windows(share, batch_count)
+    slots = Slots(micro_count, capacity)
 
     device = tower_at * batch_count + lax.axis_index("batch")
     cin_phase, rest_phase = windows.phases(device)
@@ -1147,17 +1201,17 @@
         return jnp.moveaxis(values, 1, -1).reshape(micro_count, -1, samples)
 
     requests, codes, halves = route(
-        lanes_of(shard_ids), lanes_of(local_rows), lanes_of(bag_counts), capacity, batch_count
+        lanes_of(shard_ids), lanes_of(local_rows), lanes_of(bag_counts), slots, batch_count
     )
     pooled, served, stats, cins, rests, extras = fetch(
         requests, codes, halves, embed_table, sample_weights, cin_window, rest_window, windows,
-        capacity, micro_count,
+        slots,
     )
     grad_bags, loss, g_cins, g_rests, g_extras = dense_step(
         tower_at, stats, pooled, click_labels, sample_weights, cins, rests, extras, windows
     )
     table_grad, losses, g_cin, g_rest = return_grads(
-        grad_bags, codes, halves, served, loss, g_cins, g_rests, g_extras, windows, capacity, columns
+        grad_bags, codes, halves, served, loss, g_cins, g_rests, g_extras, windows, slots, columns
     )
     g_cin = g_cin[: windows.cin_rows].reshape(-1, FIELDS, FPAD)[:, :, :FIELDS].reshape(-1)
     g_rest = g_rest[: windows.rest_rows, :HID].reshape(-1)

time: 190 us -> 182 us (0.958)
  the two profiles are of different devices: /device:TPU:30 before, /device:TPU:0 now
where the time goes in v2:
time: 182 us; the launch traced here: 180 us
  Pallas kernels  167 us (92%)
  other arithmetic  5.77 us (3%)
  local copies, waits for them, and re-layouts  3.87 us (2%)
  between operations  3.27 us (2%)
    pallas_call x1, Pallas kernels, fetch(): pl.pallas_call(partial(fetch_kernel, slots, windows, columns), in_specs=[...  69.1 us
    pallas_call x1, Pallas kernels, return_grads(): pl.pallas_call(partial(return_kernel, slots, windows, columns), in_specs=...  63.9 us
    pallas_call x1, Pallas kernels, route(): pl.pallas_call(partial(route_kernel, slots, batch_count), grid=(micro_cou...  21.7 us
    pallas_call x1, Pallas kernels, dense_step(): pl.pallas_call(partial(dense_kernel, micro_count, windows), in_specs=[in_...  12.8 us
    convert_element_type x1, other arithmetic, shards(): table_new.astype(jnp.bfloat16)  4.04 us

profile of v2, /device:TPU:0, one launch (start us, length us, event | category | flops | bytes accessed | tf_op | source)
XLA Modules:
  0.0 180.4 jit_solution(16934645750050632829)
XLA Ops:
  0.6 21.7 %route.1 = (s32[16,13,256]{2,1,0:T(8,128)S(1)}, s32[16,13,256]{2,1,0:T(8,128)S(1)}, s32[16,13,256]{2,1,0:T(8,128)S(1)}) custom-call(s32[3,80,104]{2,1,0:T(8,128)} %bitcast.15, s32[3,80,104]{2,1,0:T(8,128)} %bitcast.16, s32[3,39,104]{2,1,0:T(8,128)} %bitcast.17), custom_call_target="tpu_custom_call" | custom-call | tf_op jit(solution)/shard_map/route/pallas_call | solution.py:232
  22.3 0.9 convert_element_type.13
  23.2 0.5 dynamic_update_slice.6
  23.8 0.2 reshape.49
  24.0 0.1 reshape.50.cin_ref
  24.2 0.5 dynamic_update_slice.7
  24.7 0.1 reshape.51
  24.9 0.0 copy-start
  24.9 0.7 copy-done
  25.6 69.1 %fetch.1 = (f32[3,248,256]{2,1,0:T(8,128)S(1)}, s32[16,13,256]{2,1,0:T(8,128)S(1)}, f32[8,128]{1,0:T(8,128)S(1)}, bf16[16,16,1560]{2,1,0:T(8,128)(2,1)S(1)}, bf1...) custom-call(s32[16,13,256]{2,1,0:T(8,128)S(1)} %get-tuple-element.27.req_ref, ...), custom_call_target="tpu_custom_call" | custom-call | tf_op jit(solution)/shard_map/fetch/pallas_call | solution.py:594
  94.7 0.0 copy-done.1
  94.7 0.0 copy-start.4
  94.7 12.8 %dense.1 = (bf16[3,248,256]{2,1,0:T(8,128)(2,1)S(1)}, f32[8,128]{1,0:T(8,128)S(1)}, f32[16,16,1560]{2,1,0:T(8,128)S(1)}, f32[16,56,512]{2,1,0:T(8,128)S(1)}, f32[1,56,512]{2,1,0:T(8,128)S(1)}) custom-call(s32[1]{0:T(128)} %bitcast.tower_ref, f32[8,128]{1,0:T(8,128)S(1)} %get-tuple-element.30.stat_ref, f32[3,248,256]{2,1,0:T(8,128)S(1)} %get-tuple-element.31.pooled_ref, ...), custom_call_target="tpu_custom_call" | custom-call | tf_op jit(solution)/shard_map/dense/pallas_call | solution.py:1139
  107.6 0.0 copy-start.2
  107.6 0.0 copy-start.3
  107.6 63.9 %return_grads.1 = (f32[11,32768]{1,0:T(8,128)S(1)}, f32[8,128]{1,0:T(8,128)S(1)}, f32[16,1560]{1,0:T(8,128)S(1)}, f32[56,512]{1,0:T(8,128)S(1)}) custom-call(bf16[3,248,256]{2,1,0:T(8,128)(2,1)S(1)} %get-tuple-element.35.grad_ref, s32[16,13,256]{2,1,0:T(8,128)S(1)} %get-tuple-element.28.code_ref, s32[16,13,256]{2,1,0:T(8,128)S(1)} %get-tuple-element.29.half_ref, ...), custom_call_target="tpu_custom_call" | custom-call | tf_op jit(solution)/shard_map/return_grads/pallas_call | solution.py:876
  171.5 0.0 copy-done.4
  171.5 0.0 copy-done.2
  171.5 0.0 copy-done.3
  171.5 0.0 copy-start.5
  171.5 0.0 copy-start.6
  171.5 0.0 copy-start.7
  171.5 4.0 %fusion.4 = (bf16[11,32768]{1,0:T(8,128)(2,1)}, f32[11,32768]{1,0:T(8,128)}, f32[11,32768]{1,0:T(8,128)}, f32[11,32768]{1,0:T(8,128)}) fusion(f32[11,32768]{1,0:T(8,128)S(1)} %copy-done.2, f32[11,32768]{1,0:T(8,128)S(1)} %get-tuple-element.41, f32[11,32768]{1,0:T(8,128)S(1)} %copy-done.3, f32[11,32768]{1,0:T(8,128)S(1)} %copy-done.4), kind=kLoop, calls=%fused_computation.11 | loop fusion | flops 5767168 | bytes 10813440 | tf_op jit(solution)/shard_map/convert_element_type | solution.py:1236
  175.6 0.1 reshape.54
  175.7 0.2 reshape.52
  175.9 0.2 reshape.53
  176.1 0.0 copy-done.5
  176.1 0.0 copy-done.6
  176.1 0.0 copy-done.7
  176.1 0.8 fusion.2
  176.9 0.5 slice.18
  177.5 0.5 slice.19
  (5 shorter events, 0.1 us)
Async XLA Ops:
  23.2 71.5 %copy-start.1 = (s32[3,104]{1,0:T(4,128)S(1)}, s32[3,104]{1,0:T(4,128)}, u32[]{:S(2)}) copy-start(s32[3,104]{1,0:T(4,128)} %label_ref.1) | copy-start | bytes 3748
  24.9 0.7 copy-start
  94.7 76.7 %copy-start.4 = (f32[11,32768]{1,0:T(8,128)S(1)}, f32[11,32768]{1,0:T(8,128)}, u32[]{:S(2)}) copy-start(f32[11,32768]{1,0:T(8,128)} %param.18) | copy-start | bytes 4325380
  107.6 63.9 %copy-start.2 = (f32[11,32768]{1,0:T(8,128)S(1)}, f32[11,32768]{1,0:T(8,128)}, u32[]{:S(2)}) copy-start(f32[11,32768]{1,0:T(8,128)} %table_hbm_ref.1) | copy-start | bytes 4325380
  107.6 63.9 %copy-start.3 = (f32[11,32768]{1,0:T(8,128)S(1)}, f32[11,32768]{1,0:T(8,128)}, u32[]{:S(2)}) copy-start(f32[11,32768]{1,0:T(8,128)} %param.17) | copy-start | bytes 4325380
  171.5 4.6 %copy-start.5 = (f32[19426]{0:T(1024)S(1)}, f32[19426]{0:T(1024)}, u32[]{:S(2)}) copy-start(f32[19426]{0:T(1024)} %param.19) | copy-start | bytes 233116
  171.5 4.6 %copy-start.6 = (f32[19426]{0:T(1024)S(1)}, f32[19426]{0:T(1024)}, u32[]{:S(2)}) copy-start(f32[19426]{0:T(1024)} %param.20) | copy-start | bytes 233116
  171.5 4.6 %copy-start.7 = (f32[19426]{0:T(1024)S(1)}, f32[19426]{0:T(1024)}, u32[]{:S(2)}) copy-start(f32[19426]{0:T(1024)} %param.21) | copy-start | bytes 233116

commit v3 on v2

--- a/solution.py
+++ b/solution.py
@@ -115,8 +115,16 @@
         return start % SQUARE, jnp.mod(start - CIN_SIZE, HID)
 
 
+def coded(x):
+    return jnp.where(x < 256, x + 1, 255 - x).astype(jnp.float32)
+
+
+def decoded(x):
+    return jnp.where(x > 0, x - 1, 255 - x)
+
+
 def route_kernel(
-    slots, batch_count, ids_ref, rows_ref, counts_ref,
+    slots, batch_count, ids_ref, rows_ref, counts_ref, weight_ref,
     req_ref, code_ref, half_ref, part_ref, left_ref, right_ref,
 ):
     f32, bf16 = jnp.float32, jnp.bfloat16
@@ -132,6 +140,8 @@
         code_ref[...] = jnp.zeros_like(code_ref)
         half_ref[...] = jnp.zeros_like(half_ref)
         part_ref[...] = jnp.zeros_like(part_ref)
+        weight_sum = jnp.sum(weight_ref[...].astype(f32)).astype(jnp.int32)
+        req_ref[:, slots.rows, :] = jnp.full((batch_count, WIDE), weight_sum)
 
     def widened(x, filler):
         part_ref[0, :, :samples] = x.astype(f32)
@@ -148,8 +158,7 @@
     field = jnp.zeros((id_rows, samples), jnp.int32)
     for f in range(FIELDS):
         field = field + jnp.where(iota((id_rows, samples), 0) >= ends[f : f + 1], 1, 0)
-    field = widened(field, 0.0)
-    late = jnp.where(field >= HALF, 1.0, 0.0)
+    bag = iota((id_rows, LANES), 1) * FIELDS + widened(field, 0.0).astype(jnp.int32)
 
     earlier_rows = ones_at(iota((id_rows, id_rows), 1) < iota((id_rows, id_rows), 0))
     upper = iota((2 * LANES, LANES), 0)
@@ -175,10 +184,9 @@
     place = jnp.where(target < batch_count, (slot // WIDE) * batch_count + target, -1)
     part_ref[0] = place.astype(f32)
     part_ref[1] = (slot % WIDE).astype(f32)
-    part_ref[2] = (local // WIDE).astype(f32)
-    part_ref[3] = (local % WIDE).astype(f32)
-    part_ref[4] = late * LANES + (iota((id_rows, LANES), 1) + 1).astype(f32)
-    part_ref[5] = field - late * HALF
+    part_ref[2] = coded(local // 64)
+    part_ref[3] = coded((local % 64) * 8 + bag // 512)
+    part_ref[4] = coded(bag % 512)
     places = window * batch_count
 
     def build(t, carry):
@@ -188,7 +196,7 @@
             return part_ref[k, pl.ds(t, 1), :]
 
         mask = iota((places, LANES), 0).astype(f32) == row(0)
-        for v in range(4):
+        for v in range(3):
             left_ref[v * places : (v + 1) * places, span] = jnp.where(
                 mask, row(2 + v), 0.0
             ).astype(bf16)
@@ -210,39 +218,45 @@
                 at = slots.first_rows[m] + r
                 if slots.micro_width(m, at) == 0:
                     continue
-                code = part(2, r)
-                req_ref[:, at, :] += part(0, r) * WIDE + part(1, r)
-                code_ref[:, at, :] += jnp.where(code > 0, code + m * WIDE, 0)
-                half_ref[:, at, :] += part(3, r)
+                middle = decoded(part(1, r))
+                bag = middle % 8 * 512 + decoded(part(2, r))
+                valid = part(2, r) != 0
+                sample = ((bag.astype(f32) + 0.5) * (1.0 / FIELDS)).astype(jnp.int32)
+                field = bag - sample * FIELDS
+                late = jnp.where(field >= HALF, 1, 0)
+                code = sample + late * LANES + (m * WIDE + 1)
+                row = decoded(part(0, r)) * 64 + middle // 8
+                req_ref[:, at, :] += jnp.where(valid, row, 0)
+                code_ref[:, at, :] += jnp.where(valid, code, 0)
+                half_ref[:, at, :] += jnp.where(valid, field - late * HALF, 0)
 
 
 def in_hbm(x):
     return pltpu.with_memory_space_constraint(x, pltpu.HBM)
 
 
-def route(ids, rows, counts, slots, batch_count):
+def route(ids, rows, counts, weights, slots, batch_count):
     micro_count, id_rows, samples = ids.shape
     places = slots.window * batch_count
 
     def block(x):
         return pl.BlockSpec((1,) + x.shape[1:], lambda m: (m, 0, 0))
 
-    whole = pl.BlockSpec((batch_count, slots.rows, WIDE), lambda m: (0, 0, 0))
-    shape = jax.ShapeDtypeStruct((batch_count, slots.rows, WIDE), jnp.int32)
+    shapes = [(batch_count, slots.rows + k, WIDE) for k in (1, 0, 0)]
     return pl.pallas_call(
         partial(route_kernel, slots, batch_count),
         grid=(micro_count,),
-        in_specs=[block(ids), block(rows), block(counts)],
-        out_specs=[whole] * 3,
-        out_shape=[shape] * 3,
+        in_specs=[block(ids), block(rows), block(counts), pl.BlockSpec(weights.shape, lambda m: (0, 0))],
+        out_specs=[pl.BlockSpec(shape, lambda m: (0, 0, 0)) for shape in shapes],
+        out_shape=[jax.ShapeDtypeStruct(shape, jnp.int32) for shape in shapes],
         scratch_shapes=[
-            pltpu.VMEM((6, id_rows, LANES), jnp.float32),
-            pltpu.VMEM((4 * places, id_rows * LANES), jnp.bfloat16),
+            pltpu.VMEM((5, id_rows, LANES), jnp.float32),
+            pltpu.VMEM((3 * places, id_rows * LANES), jnp.bfloat16),
             pltpu.VMEM((WIDE, id_rows * LANES), jnp.bfloat16),
         ],
         compiler_params=pltpu.CompilerParams(vmem_limit_bytes=vmem_limit(batch_count)),
         name="route",
-    )(in_hbm(ids), in_hbm(rows), in_hbm(counts))
+    )(in_hbm(ids), in_hbm(rows), in_hbm(counts), weights)
 
 
 def peer_copy(src, dst, send_sem, recv_sem, peer):
@@ -283,7 +297,7 @@
 
 
 def message_rows(rows_msg, columns):
-    return -(-rows_msg * columns // 16) * 16
+    return -(-(rows_msg * columns + 1) // 16) * 16
 
 
 def each(count, action):
@@ -314,11 +328,11 @@
 
 def fetch_kernel(
     slots, windows, columns,
-    req_ref, code_ref, half_ref, table_hbm_ref, weight_ref, cin_ref, rest_ref,
+    req_ref, code_ref, half_ref, table_hbm_ref, cin_ref, rest_ref,
     out_ref, served_ref, stat_out_ref, cins_ref, rests_ref, extras_ref,
     table_ref, tiles_ref, stage_ref, first_ref, second_ref, ans_out_ref, ans_in_ref, left_ref, pooled_ref,
-    other_ref, stat_ref, stat_in_ref,
-    req_send, req_recv, ans_send, ans_recv, stat_send, stat_recv, win_send, win_recv, plane_send,
+    other_ref,
+    req_send, req_recv, ans_send, ans_recv, win_send, win_recv, plane_send,
     plane_recv, ext_send, ext_recv, pair_send, pair_recv, table_sem,
 ):
     rows_msg = slots.rows
@@ -339,11 +353,6 @@
             req_ref.at[peer], served_ref.at[slot], req_send.at[peer], req_recv.at[slot], peer
         )
 
-    stat_ref[...] = jnp.full(stat_ref.shape, jnp.sum(weight_ref[...].astype(jnp.float32)))
-
-    def stat_copy(peer, slot):
-        return peer_copy(stat_ref, stat_in_ref.at[slot], stat_send.at[peer], stat_recv.at[slot], peer)
-
     def answer_copy(peer, slot):
         return peer_copy(
             ans_out_ref.at[peer], ans_in_ref.at[slot], ans_send.at[peer], ans_recv.at[slot], peer
@@ -357,7 +366,6 @@
     def send_requests(i, carry):
         peer = lax.rem(me + i, batch_count)
         request_copy(peer, me).start()
-        stat_copy(peer, me).start()
         return carry
 
     lax.fori_loop(1, batch_count, send_requests, 0)
@@ -411,7 +419,6 @@
             action(rest_ref, rests_ref)
 
     served_ref[me] = req_ref[me]
-    stat_in_ref[me] = stat_ref[...]
     load_table.wait()
     tile_table(table_ref, tiles_ref, stage_ref, columns)
 
@@ -432,7 +439,7 @@
         ans_out_ref[first] = first_ref[:sizes, :].astype(jnp.bfloat16)
         ans_out_ref[second] = second_ref[:sizes, :].astype(jnp.bfloat16)
 
-    def pool(owner):
+    def pool(owner, after=None):
         first_ref[:sizes, :] = ans_in_ref[owner].astype(jnp.float32)
         for r in range(rows_msg):
             w = slots.width(r)
@@ -455,6 +462,8 @@
             pooled_ref[m] += dot(
                 left_ref[:, begin : begin + slots.spans[m]], jnp.concatenate(rights, axis=1), NT
             )
+            if after is not None:
+                after(m)
 
     def pair_copy(src, dst, k):
         return pltpu.make_async_remote_copy(
@@ -543,22 +552,21 @@
 
     lax.fori_loop(0, pairs + lag, step, 0)
 
+    def pooled_copy(m):
+        return pair_copy(pooled_ref.at[m], other_ref.at[m], 2 + m)
+
     own_copy().wait()
-    pool(me)
-
-    pooled_pair = pair_copy(pooled_ref, other_ref, 2)
-    pooled_pair.start()
+    pool(me, lambda m: pooled_copy(m).start())
 
     def finish(i, carry):
         peer = lax.rem(me + i, batch_count)
         request_copy(peer, me).wait_send()
-        stat_copy(peer, me).wait_send()
         answer_copy(peer, me).wait_send()
-        stat_copy(peer, peer).wait_recv()
         return carry
 
     lax.fori_loop(1, batch_count, finish, 0)
-    stat_out_ref[...] = jnp.sum(stat_in_ref[...], axis=0)
+    weight_sum = jnp.sum(served_ref[:, rows_msg, :LANES], axis=0, keepdims=True)
+    stat_out_ref[...] = jnp.broadcast_to(weight_sum.astype(jnp.float32), stat_out_ref.shape)
 
     split(sent_windows)
 
@@ -578,14 +586,15 @@
         pair_copy(cins_ref, cins_ref, 0).wait_recv()
         pair_copy(extras_ref, extras_ref, 1).wait_recv()
 
-    pooled_pair.wait()
-    out_ref[...] = pooled_ref[...] + other_ref[...]
+    for m in range(slots.micro_count):
+        pooled_copy(m).wait()
+        out_ref[m] = pooled_ref[m] + other_ref[m]
 
 
 def fetch(
-    requests, codes, halves, table, weights, cin_window, rest_window, windows, slots
+    requests, codes, halves, table, cin_window, rest_window, windows, slots
 ):
-    batch_count, rows_msg, _ = requests.shape
+    batch_count, rows_msg, _ = codes.shape
     columns, rows_dev = table.shape
     sizes = message_rows(rows_msg, columns)
     in_vmem = pl.BlockSpec(memory_space=pltpu.VMEM)
@@ -593,7 +602,7 @@
     bags = (slots.micro_count, BAG_ROWS, WIDE)
     return pl.pallas_call(
         partial(fetch_kernel, slots, windows, columns),
-        in_specs=[in_vmem] * 3 + [pl.BlockSpec(memory_space=pltpu.HBM)] + [in_vmem] * 3,
+        in_specs=[in_vmem] * 3 + [pl.BlockSpec(memory_space=pltpu.HBM)] + [in_vmem] * 2,
         out_specs=[in_vmem] * 6,
         out_shape=[
             jax.ShapeDtypeStruct(bags, jnp.float32),
@@ -614,25 +623,23 @@
             pltpu.VMEM((BAG_ROWS, rows_msg * WIDE), jnp.bfloat16),
             pltpu.VMEM(bags, jnp.float32),
             pltpu.VMEM(bags, jnp.float32),
-            pltpu.VMEM((8, LANES), jnp.float32),
-            pltpu.VMEM((batch_count, 8, LANES), jnp.float32),
         ]
-        + [dma((batch_count,))] * 11
-        + [dma((windows.extras,)), dma((3,)), dma((3,)), dma],
+        + [dma((batch_count,))] * 9
+        + [dma((windows.extras,)), dma((2 + slots.micro_count,)), dma((2 + slots.micro_count,)), dma],
         compiler_params=pltpu.CompilerParams(
             vmem_limit_bytes=vmem_limit(batch_count), collective_id=0, has_side_effects=True
         ),
         name="fetch",
-    )(requests, codes, halves, in_hbm(table), weights, cin_window, rest_window)
+    )(requests, codes, halves, in_hbm(table), cin_window, rest_window)
 
 
 def return_kernel(
     slots, windows, columns,
     grad_ref, code_ref, half_ref, served_ref, stat_ref, cins_ref, rests_ref, extras_ref,
     out_ref, stat_out_ref, cin_ref, rest_ref,
-    send_ref, recv_ref, first_ref, second_ref, left_ref, right_ref, total_ref, stat_in_ref,
+    send_ref, recv_ref, first_ref, second_ref, left_ref, right_ref, total_ref,
     extra_in_ref, cin_near_ref, cin_sum_ref, cin_far_ref, rest_near_ref, rest_sum_ref, rest_far_ref,
-    val_send, val_recv, stat_send, stat_recv, win_send, win_recv, plane_send, plane_recv, ext_send,
+    val_send, val_recv, win_send, win_recv, plane_send, plane_recv, ext_send,
     ext_recv,
 ):
     batch_count = windows.batch_count
@@ -650,9 +657,6 @@
     def own_copy():
         return pltpu.make_async_copy(send_ref.at[me], recv_ref.at[me], val_recv.at[me])
 
-    def stat_copy(peer, slot):
-        return peer_copy(stat_ref, stat_in_ref.at[slot], stat_send.at[peer], stat_recv.at[slot], peer)
-
     depth = batch_count // PLANE
     high, low = me // PLANE, lax.rem(me, PLANE)
 
@@ -710,13 +714,15 @@
             peer,
         )
 
-    def send_stats(i, carry):
-        stat_copy(lax.rem(me + i, batch_count), me).start()
-        return carry
-
     first_ref[...] = jnp.zeros_like(first_ref)
     second_ref[...] = jnp.zeros_like(second_ref)
-    stat_in_ref[me] = stat_ref[...]
+    spare = rows_msg * columns
+    loss_parts = split_three(stat_ref[0:1, :])
+    loss_row = sum(
+        jnp.where(iota((1, LANES), 1) == k, part.astype(jnp.float32), 0.0)
+        for k, part in enumerate(loss_parts)
+    )
+    stat_out_ref[...] = jnp.zeros_like(stat_out_ref)
     total_ref[...] = jnp.zeros_like(total_ref)
 
     sizes = send_ref.shape[1]
@@ -746,11 +752,14 @@
             block = jnp.where(iota((16, 2 * w), 0) == EMB, linear, block)
             first_ref[r * columns : r * columns + 16, :w] = block[:, :w]
             second_ref[r * columns : r * columns + 16, :w] = block[:, w:]
+        first_ref[spare : spare + 1, :LANES] = loss_row
+        second_ref[spare : spare + 1, :LANES] = loss_row
         send_ref[first] = first_ref[:sizes, :].astype(jnp.bfloat16)
         send_ref[second] = second_ref[:sizes, :].astype(jnp.bfloat16)
 
     def scatter(source):
         first_ref[:sizes, :] = recv_ref[source].astype(jnp.float32)
+        stat_out_ref[0:1, :] += first_ref[spare : spare + 1, :LANES]
         for r in range(rows_msg):
             w = slots.width(r)
             span = slice(r * WIDE, r * WIDE + w)
@@ -778,7 +787,6 @@
             @pl.when(j == 0)
             def _():
                 all_greeted(batch_count, False)
-                lax.fori_loop(1, batch_count, send_stats, 0)
 
             value_copy(first, me).start()
 
@@ -851,12 +859,11 @@
     def finish(i, carry):
         peer = lax.rem(me + i, batch_count)
         value_copy(peer, me).wait_send()
-        stat_copy(peer, me).wait_send()
-        stat_copy(peer, peer).wait_recv()
         return carry
 
     lax.fori_loop(1, batch_count, finish, 0)
-    stat_out_ref[...] = jnp.sum(stat_in_ref[...], axis=0)
+    losses = jnp.sum(stat_out_ref[0:1, :], axis=1, keepdims=True)
+    stat_out_ref[...] = jnp.broadcast_to(losses, stat_out_ref.shape)
     for c in range(columns):
         for q in range(TALL):
             out_ref[c : c + 1, q * BROAD : (q + 1) * BROAD] = total_ref[
@@ -891,7 +898,6 @@
             pltpu.VMEM((columns * TALL, long), jnp.bfloat16),
             pltpu.VMEM((BROAD, long), jnp.bfloat16),
             pltpu.VMEM((columns * TALL, BROAD), jnp.float32),
-            pltpu.VMEM((batch_count,) + stat.shape, jnp.float32),
             pltpu.VMEM(rests.shape, jnp.float32),
         ]
         + [
@@ -899,7 +905,7 @@
             for x in (cins, rests)
             for lead in ((PLANE, depth), (depth,), (depth,))
         ]
-        + [dma((batch_count,))] * 10,
+        + [dma((batch_count,))] * 8,
         compiler_params=pltpu.CompilerParams(
             vmem_limit_bytes=vmem_limit(batch_count), collective_id=1, has_side_effects=True
         ),
@@ -1201,11 +1207,11 @@
         return jnp.moveaxis(values, 1, -1).reshape(micro_count, -1, samples)
 
     requests, codes, halves = route(
-        lanes_of(shard_ids), lanes_of(local_rows), lanes_of(bag_counts), slots, batch_count
+        lanes_of(shard_ids), lanes_of(local_rows), lanes_of(bag_counts), sample_weights,
+        slots, batch_count,
     )
     pooled, served, stats, cins, rests, extras = fetch(
-        requests, codes, halves, embed_table, sample_weights, cin_window, rest_window, windows,
-        slots,
+        requests, codes, halves, embed_table, cin_window, rest_window, windows, slots
     )
     grad_bags, loss, g_cins, g_rests, g_extras = dense_step(
         tower_at, stats, pooled, click_labels, sample_weights, cins, rests, extras, windows

time: 182 us -> 179 us (0.984)
  Pallas kernels: 167 us -> 164 us
    pallas_call x1, Pallas kernels: 21.7 us -> 19.4 us  [route(): pl.pallas_call(partial(route_kernel, slots, batch_count), grid=(micro_cou...]
where the time goes in v3:
time: 179 us; the launch traced here: 177 us
  Pallas kernels  164 us (92%)
  other arithmetic  5.77 us (3%)
  local copies, waits for them, and re-layouts  3.91 us (2%)
  between operations  3.35 us (2%)
    pallas_call x1, Pallas kernels, fetch(): pl.pallas_call(partial(fetch_kernel, slots, windows, columns), in_specs=[...  69.1 us
    pallas_call x1, Pallas kernels, return_grads(): pl.pallas_call(partial(return_kernel, slots, windows, columns), in_specs=...  62.5 us
    pallas_call x1, Pallas kernels, route(): pl.pallas_call(partial(route_kernel, slots, batch_count), grid=(micro_cou...  19.4 us
    pallas_call x1, Pallas kernels, dense_step(): pl.pallas_call(partial(dense_kernel, micro_count, windows), in_specs=[in_...  12.8 us
    convert_element_type x1, other arithmetic, shards(): table_new.astype(jnp.bfloat16)  4.04 us

profile of v3, /device:TPU:0, one launch (start us, length us, event | category | flops | bytes accessed | tf_op | source)
XLA Modules:
  0.0 176.9 jit_solution(4170674163121100500)
XLA Ops:
  0.6 0.0 copy-start
  0.7 0.7 copy-done
  1.3 19.4 %route.1 = (s32[16,14,256]{2,1,0:T(8,128)S(1)}, s32[16,13,256]{2,1,0:T(8,128)S(1)}, s32[16,13,256]{2,1,0:T(8,128)S(1)}) custom-call(s32[3,80,104]{2,1,0:T(8,128)} %bitcast.15, s32[3,80,104]{2,1,0:T(8,128)} %bitcast.16, s32[3,39,104]{2,1,0:T(8,128)} %bitcast.17, s32[3,104]{1,0:T(4,128)S(1)} %copy-done), custom_call_target="tpu_custom_call" | custom-call | tf_op jit(solution)/shard_map/route/pallas_call | solution.py:246
  20.7 0.9 convert_element_type.13
  21.6 0.5 dynamic_update_slice.6
  22.2 0.2 reshape.49
  22.5 0.1 reshape.50.cin_ref
  22.6 0.5 dynamic_update_slice.7
  23.2 0.1 reshape.51
  23.3 69.1 %fetch.1 = (f32[3,248,256]{2,1,0:T(8,128)S(1)}, s32[16,14,256]{2,1,0:T(8,128)S(1)}, f32[8,128]{1,0:T(8,128)S(1)}, bf16[16,16,1560]{2,1,0:T(8,128)(2,1)S(1)}, bf1...) custom-call(s32[16,14,256]{2,1,0:T(8,128)S(1)} %get-tuple-element.27.req_ref, ...), custom_call_target="tpu_custom_call" | custom-call | tf_op jit(solution)/shard_map/fetch/pallas_call | solution.py:603
  92.5 0.0 copy-done.1
  92.5 0.0 copy-done.2
  92.5 0.0 copy-start.5
  92.5 12.8 %dense.1 = (bf16[3,248,256]{2,1,0:T(8,128)(2,1)S(1)}, f32[8,128]{1,0:T(8,128)S(1)}, f32[16,16,1560]{2,1,0:T(8,128)S(1)}, f32[16,56,512]{2,1,0:T(8,128)S(1)}, f32[1,56,512]{2,1,0:T(8,128)S(1)}) custom-call(s32[1]{0:T(128)} %bitcast.tower_ref, f32[8,128]{1,0:T(8,128)S(1)} %get-tuple-element.30.stat_ref, f32[3,248,256]{2,1,0:T(8,128)S(1)} %get-tuple-element.31.pooled_ref, ...), custom_call_target="tpu_custom_call" | custom-call | tf_op jit(solution)/shard_map/dense/pallas_call | solution.py:1145
  105.3 0.0 copy-start.3
  105.3 0.0 copy-start.4
  105.4 62.5 %return_grads.1 = (f32[11,32768]{1,0:T(8,128)S(1)}, f32[8,128]{1,0:T(8,128)S(1)}, f32[16,1560]{1,0:T(8,128)S(1)}, f32[56,512]{1,0:T(8,128)S(1)}) custom-call(bf16[3,248,256]{2,1,0:T(8,128)(2,1)S(1)} %get-tuple-element.35.grad_ref, s32[16,13,256]{2,1,0:T(8,128)S(1)} %get-tuple-element.28.code_ref, s32[16,13,256]{2,1,0:T(8,128)S(1)} %get-tuple-element.29.half_ref, ...), custom_call_target="tpu_custom_call" | custom-call | tf_op jit(solution)/shard_map/return_grads/pallas_call | solution.py:883
  167.9 0.0 copy-done.5
  167.9 0.0 copy-done.3
  167.9 0.0 copy-done.4
  167.9 0.0 copy-start.6
  168.0 0.0 copy-start.7
  168.0 0.0 copy-start.8
  168.0 4.0 %fusion.4 = (bf16[11,32768]{1,0:T(8,128)(2,1)}, f32[11,32768]{1,0:T(8,128)}, f32[11,32768]{1,0:T(8,128)}, f32[11,32768]{1,0:T(8,128)}) fusion(f32[11,32768]{1,0:T(8,128)S(1)} %copy-done.3, f32[11,32768]{1,0:T(8,128)S(1)} %get-tuple-element.41, f32[11,32768]{1,0:T(8,128)S(1)} %copy-done.4, f32[11,32768]{1,0:T(8,128)S(1)} %copy-done.5), kind=kLoop, calls=%fused_computation.11 | loop fusion | flops 5767168 | bytes 10813440 | tf_op jit(solution)/shard_map/convert_element_type | solution.py:1242
  172.0 0.1 reshape.54
  172.1 0.2 reshape.52
  172.3 0.2 reshape.53
  172.5 0.0 copy-done.6
  172.5 0.0 copy-done.7
  172.6 0.8 fusion.2
  173.4 0.5 slice.18
  173.9 0.5 slice.19
  (7 shorter events, 0.1 us)
Async XLA Ops:
  0.6 0.7 copy-start
  21.6 70.9 %copy-start.1 = (s32[3,104]{1,0:T(4,128)S(1)}, s32[3,104]{1,0:T(4,128)}, u32[]{:S(2)}) copy-start(s32[3,104]{1,0:T(4,128)} %weight_ref.3) | copy-start | bytes 3748
  21.6 70.9 %copy-start.2 = (s32[3,104]{1,0:T(4,128)S(1)}, s32[3,104]{1,0:T(4,128)}, u32[]{:S(2)}) copy-start(s32[3,104]{1,0:T(4,128)} %label_ref.1) | copy-start | bytes 3748
  92.5 75.4 %copy-start.5 = (f32[11,32768]{1,0:T(8,128)S(1)}, f32[11,32768]{1,0:T(8,128)}, u32[]{:S(2)}) copy-start(f32[11,32768]{1,0:T(8,128)} %param.18) | copy-start | bytes 4325380
  105.3 62.6 %copy-start.3 = (f32[11,32768]{1,0:T(8,128)S(1)}, f32[11,32768]{1,0:T(8,128)}, u32[]{:S(2)}) copy-start(f32[11,32768]{1,0:T(8,128)} %table_hbm_ref.1) | copy-start | bytes 4325380
  105.3 62.6 %copy-start.4 = (f32[11,32768]{1,0:T(8,128)S(1)}, f32[11,32768]{1,0:T(8,128)}, u32[]{:S(2)}) copy-start(f32[11,32768]{1,0:T(8,128)} %param.17) | copy-start | bytes 4325380
  167.9 4.6 %copy-start.6 = (f32[19426]{0:T(1024)S(1)}, f32[19426]{0:T(1024)}, u32[]{:S(2)}) copy-start(f32[19426]{0:T(1024)} %param.19) | copy-start | bytes 233116
  168.0 4.6 %copy-start.7 = (f32[19426]{0:T(1024)S(1)}, f32[19426]{0:T(1024)}, u32[]{:S(2)}) copy-start(f32[19426]{0:T(1024)} %param.20) | copy-start | bytes 233116
  168.0 4.6 %copy-start.8 = (f32[19426]{0:T(1024)S(1)}, f32[19426]{0:T(1024)}, u32[]{:S(2)}) copy-start(f32[19426]{0:T(1024)} %param.21) | copy-start | bytes 233116

commit v4 on v3

--- a/solution.py
+++ b/solution.py
@@ -329,8 +329,8 @@
 def fetch_kernel(
     slots, windows, columns,
     req_ref, code_ref, half_ref, table_hbm_ref, cin_ref, rest_ref,
-    out_ref, served_ref, stat_out_ref, cins_ref, rests_ref, extras_ref,
-    table_ref, tiles_ref, stage_ref, first_ref, second_ref, ans_out_ref, ans_in_ref, left_ref, pooled_ref,
+    out_ref, served_ref, stat_out_ref, cin_full_ref, rest_full_ref,
+    cins_ref, rests_ref, extras_ref, table_ref, tiles_ref, stage_ref, first_ref, second_ref, ans_out_ref, ans_in_ref, left_ref, pooled_ref,
     other_ref,
     req_send, req_recv, ans_send, ans_recv, win_send, win_recv, plane_send,
     plane_recv, ext_send, ext_recv, pair_send, pair_recv, table_sem,
@@ -358,9 +358,6 @@
             ans_out_ref.at[peer], ans_in_ref.at[slot], ans_send.at[peer], ans_recv.at[slot], peer
         )
 
-    def own_copy():
-        return pltpu.make_async_copy(ans_out_ref.at[me], ans_in_ref.at[me], ans_recv.at[me])
-
     all_greeted(batch_count, True)
 
     def send_requests(i, carry):
@@ -438,6 +435,21 @@
             second_ref[r * columns : r * columns + 16, :w] = block[:, w:]
         ans_out_ref[first] = first_ref[:sizes, :].astype(jnp.bfloat16)
         ans_out_ref[second] = second_ref[:sizes, :].astype(jnp.bfloat16)
+
+    def look_up_one(source):
+        half = rows_msg // 2
+        for r in range(half + rows_msg % 2):
+            both = [r, r + half] if r < half else [rows_msg - 1]
+            widths = [slots.width(x) for x in both]
+            row = jnp.concatenate(
+                [served_ref[source, x : x + 1, :w] for x, w in zip(both, widths)], axis=1
+            )
+            hot = ones_at(iota((BROAD, row.shape[1]), 0) == row % BROAD)
+            result = dot(tiles_ref[...], hot)
+            mask = iota((TALL, row.shape[1]), 0) == row // BROAD
+            block = pick_rows(result, mask, TALL, columns)
+            for at, x, w in zip((0, WIDE), both, widths):
+                first_ref[x * columns : (x + 1) * columns, :w] = block[:columns, at : at + w]
 
     def pool(owner, after=None):
         first_ref[:sizes, :] = ans_in_ref[owner].astype(jnp.float32)
@@ -496,55 +508,65 @@
     pairs = batch_count // 2
     lag = 2
 
+    last = lax.rem(me + 1, batch_count)
+
     def step(j, carry):
-        @pl.when(j < pairs)
-        def _():
-            first = lax.rem(me + batch_count - (2 * j + 1), batch_count)
-            second = lax.rem(me + 2 * batch_count - (2 * j + 2), batch_count)
-            request_copy(first, first).wait_recv()
-
-            @pl.when(j < pairs - 1)
+        @pl.when((j == 0) | (j == pairs))
+        def _():
+            @pl.when(j == pairs)
             def _():
-                request_copy(second, second).wait_recv()
-
-            look_up(first, second)
+                request_copy(last, last).wait_recv()
+
+            look_up_one(jnp.where(j == 0, me, last))
 
             @pl.when(j == 0)
             def _():
+                ans_in_ref[me] = first_ref[:sizes, :].astype(jnp.bfloat16)
                 split(start_windows)
 
-            @pl.when((j == 0) & (tower == 0) & (me >= first_extra))
+            @pl.when(j == pairs)
             def _():
-                others(lambda peer: extra_copy(peer, me - first_extra).start())
-                extras_ref[me - first_extra] = rest_ref[...]
-
-            @pl.when(j == 3)
+                ans_out_ref[last] = first_ref[:sizes, :].astype(jnp.bfloat16)
+                answer_copy(last, me).start()
+
+        @pl.when((j == 0) & (tower == 0) & (me >= first_extra))
+        def _():
+            others(lambda peer: extra_copy(peer, me - first_extra).start())
+            extras_ref[me - first_extra] = rest_ref[...]
+
+        @pl.when((j > 0) & (j < pairs))
+        def _():
+            first = lax.rem(me + batch_count - (2 * j - 1), batch_count)
+            second = lax.rem(me + batch_count - 2 * j, batch_count)
+            request_copy(first, first).wait_recv()
+            request_copy(second, second).wait_recv()
+            look_up(first, second)
+            answer_copy(first, me).start()
+            answer_copy(second, me).start()
+
+        @pl.when(j == 3)
+        def _():
+            split(pass_windows)
+
+        @pl.when(j == pairs - 2)
+        def _():
+            swap_windows()
+
+        ready = j - lag
+
+        @pl.when((ready >= 0) & (ready < pairs))
+        def _():
+            first = lax.rem(me + batch_count + 2 * ready - 1, batch_count)
+
+            @pl.when(ready > 0)
             def _():
-                split(pass_windows)
-
-            @pl.when(j == pairs - 2)
-            def _():
-                swap_windows()
-
-            answer_copy(first, me).start()
-
-            @pl.when(j < pairs - 1)
-            def _():
-                answer_copy(second, me).start()
-
-            @pl.when(j == pairs - 1)
-            def _():
-                own_copy().start()
-
-        @pl.when(j >= lag)
-        def _():
-            first = lax.rem(me + 2 * (j - lag) + 1, batch_count)
-            answer_copy(first, first).wait_recv()
-            pool(first)
-
-        @pl.when((j >= lag) & (j < pairs - 1 + lag))
-        def _():
-            second = lax.rem(me + 2 * (j - lag) + 2, batch_count)
+                answer_copy(first, first).wait_recv()
+
+            pool(jnp.where(ready == 0, me, first))
+
+        @pl.when((ready > 0) & (ready < pairs))
+        def _():
+            second = lax.rem(me + 2 * ready, batch_count)
             answer_copy(second, second).wait_recv()
             pool(second)
 
@@ -555,8 +577,9 @@
     def pooled_copy(m):
         return pair_copy(pooled_ref.at[m], other_ref.at[m], 2 + m)
 
-    own_copy().wait()
-    pool(me, lambda m: pooled_copy(m).start())
+    final = lax.rem(me + batch_count - 1, batch_count)
+    answer_copy(final, final).wait_recv()
+    pool(final, lambda m: pooled_copy(m).start())
 
     def finish(i, carry):
         peer = lax.rem(me + i, batch_count)
@@ -586,6 +609,20 @@
         pair_copy(cins_ref, cins_ref, 0).wait_recv()
         pair_copy(extras_ref, extras_ref, 1).wait_recv()
 
+    cin_full_ref[...] = jnp.zeros_like(cin_full_ref)
+    for b, at in enumerate(windows.cin_at):
+        block = cins_ref[windows.slots[b]].astype(jnp.float32)
+        cin_full_ref[at : at + windows.cin_rows, :] += block[: windows.cin_rows]
+    rest_full_ref[...] = jnp.zeros_like(rest_full_ref)
+    pieces = [(rests_ref, windows.slots[b], at) for b, at in enumerate(windows.rest_at)]
+    pieces += [(extras_ref, e, at) for e, at in enumerate(windows.extra_at)]
+    for source, b, at in pieces:
+        skip = max(0, -at)
+        block = source[b].astype(jnp.float32)
+        for l in range(HPAD // LANES):
+            rest_full_ref[l, at + skip : at + windows.rest_rows, :] += block[
+                skip : windows.rest_rows, l * LANES : (l + 1) * LANES
+            ]
     for m in range(slots.micro_count):
         pooled_copy(m).wait()
         out_ref[m] = pooled_ref[m] + other_ref[m]
@@ -603,16 +640,18 @@
     return pl.pallas_call(
         partial(fetch_kernel, slots, windows, columns),
         in_specs=[in_vmem] * 3 + [pl.BlockSpec(memory_space=pltpu.HBM)] + [in_vmem] * 2,
-        out_specs=[in_vmem] * 6,
+        out_specs=[in_vmem] * 5,
         out_shape=[
             jax.ShapeDtypeStruct(bags, jnp.float32),
             jax.ShapeDtypeStruct(requests.shape, jnp.int32),
             jax.ShapeDtypeStruct((8, LANES), jnp.float32),
-            jax.ShapeDtypeStruct((batch_count,) + cin_window.shape, jnp.bfloat16),
-            jax.ShapeDtypeStruct((batch_count,) + rest_window.shape, jnp.bfloat16),
-            jax.ShapeDtypeStruct((windows.extras,) + rest_window.shape, jnp.bfloat16),
+            jax.ShapeDtypeStruct((windows.cin_total, PAIRS), jnp.float32),
+            jax.ShapeDtypeStruct((HPAD // LANES, windows.rest_total, LANES), jnp.float32),
         ],
         scratch_shapes=[
+            pltpu.VMEM((batch_count,) + cin_window.shape, jnp.bfloat16),
+            pltpu.VMEM((batch_count,) + rest_window.shape, jnp.bfloat16),
+            pltpu.VMEM((windows.extras,) + rest_window.shape, jnp.bfloat16),
             pltpu.VMEM(table.shape, jnp.float32),
             pltpu.VMEM((columns * TALL, BROAD), jnp.bfloat16),
             pltpu.VMEM((TALL, BROAD), jnp.float32),
@@ -923,29 +962,14 @@
 
 def dense_kernel(
     micro_count, windows, tower_ref, stat_ref, pooled_ref, label_ref, weight_ref,
-    cins_ref, rests_ref, extras_ref,
+    cin_ref, rest_ref,
     bags_ref, loss_ref, g_cins_ref, g_rests_ref, g_extras_ref,
-    embed_ref, total_ref, pairs_ref, sym_ref, cin_ref, rest_ref, lane_ref,
+    embed_ref, total_ref, pairs_ref, sym_ref, g_cin_ref, g_rest_ref, lane_ref,
 ):
     f32 = jnp.float32
     bf16 = jnp.bfloat16
     width = micro_count * LANES
     groups = HPAD // LANES
-
-    cin_ref[...] = jnp.zeros_like(cin_ref)
-    for b, at in enumerate(windows.cin_at):
-        block = cins_ref[windows.slots[b]].astype(f32)
-        cin_ref[at : at + windows.cin_rows, :] += block[: windows.cin_rows]
-    rest_ref[...] = jnp.zeros_like(rest_ref)
-    pieces = [(rests_ref, windows.slots[b], at) for b, at in enumerate(windows.rest_at)]
-    pieces += [(extras_ref, e, at) for e, at in enumerate(windows.extra_at)]
-    for source, b, at in pieces:
-        skip = max(0, -at)
-        block = source[b].astype(f32)
-        for l in range(groups):
-            rest_ref[l, at + skip : at + windows.rest_rows, :] += block[
-                skip : windows.rest_rows, l * LANES : (l + 1) * LANES
-            ]
 
     def rest_rows(begin, count):
         return jnp.concatenate(
@@ -1078,17 +1102,17 @@
     def row_sum(x):
         return sum(dot(ones, third, NT) for third in split_three(x))[:1]
 
-    rest_ref[...] = jnp.zeros_like(rest_ref)
+    g_rest_ref[...] = jnp.zeros_like(g_rest_ref)
 
     def put(begin, count, value, stride=None):
         for l in range(groups):
             piece = value[:, l * LANES : min((l + 1) * LANES, HID)]
             lanes = slice(0, piece.shape[1])
             if stride is None:
-                rest_ref[l, begin : begin + count, lanes] = piece
+                g_rest_ref[l, begin : begin + count, lanes] = piece
             else:
                 piece = jnp.pad(piece, ((0, 0), (0, LANES - piece.shape[1])))
-                rest_ref[l, pl.ds(begin, count, stride=stride), :] = piece
+                g_rest_ref[l, pl.ds(begin, count, stride=stride), :] = piece
 
     g_w_one = dot(flat, grad_one, NT)
     for d in range(EMB):
@@ -1096,20 +1120,20 @@
 
     @pl.when(tower_ref[0] == 0)
     def _():
-        cin_ref[...] = jnp.zeros_like(cin_ref)
-        cin_ref[:MAPS, :] = sum(dot(grad_maps, third, NT) for third in thirds)
+        g_cin_ref[...] = jnp.zeros_like(g_cin_ref)
+        g_cin_ref[:MAPS, :] = sum(dot(grad_maps, third, NT) for third in thirds)
         g_cin_u = jnp.sum(map_sum * grad_logits, axis=1, keepdims=True)
         thirds_u = split_three(jnp.broadcast_to(g_cin_u, (MAPS, 8)))
-        cin_ref[MAPS : MAPS + 1, :] = sum(dot(third, picks_u, TN) for third in thirds_u)[:1]
+        g_cin_ref[MAPS : MAPS + 1, :] = sum(dot(third, picks_u, TN) for third in thirds_u)[:1]
         for b, at in enumerate(windows.cin_at):
-            g_cins_ref[windows.slots[b], : windows.cin_rows, :] = cin_ref[
+            g_cins_ref[windows.slots[b], : windows.cin_rows, :] = g_cin_ref[
                 at : at + windows.cin_rows, :
             ]
         for e, at in enumerate(windows.extra_at):
             skip = max(0, -at)
             for l in range(groups):
                 span = slice(l * LANES, (l + 1) * LANES)
-                g_extras_ref[e, skip : windows.rest_rows, span] = rest_ref[
+                g_extras_ref[e, skip : windows.rest_rows, span] = g_rest_ref[
                     l, at + skip : at + windows.rest_rows, :
                 ]
 
@@ -1124,12 +1148,12 @@
         for b, at in enumerate(windows.rest_at):
             for l in range(groups):
                 span = slice(l * LANES, (l + 1) * LANES)
-                g_rests_ref[windows.slots[b], : windows.rest_rows, span] = rest_ref[
+                g_rests_ref[windows.slots[b], : windows.rest_rows, span] = g_rest_ref[
                     l, at : at + windows.rest_rows, :
                 ]
 
 
-def dense_step(tower_at, stats, pooled, labels, weights, cins, rests, extras, windows):
+def dense_step(tower_at, stats, pooled, labels, weights, cin_full, rest_full, windows):
     micro_count = pooled.shape[0]
     width = micro_count * LANES
     in_vmem = pl.BlockSpec(memory_space=pltpu.VMEM)
@@ -1138,13 +1162,13 @@
     shapes = [
         ((micro_count, BAG_ROWS, WIDE), jnp.bfloat16),
         ((8, LANES), f32),
-        ((cins.shape[0], windows.cin_pad_wide, PAIRS), f32),
-        ((rests.shape[0], windows.rest_pad_wide, HPAD), f32),
-        ((extras.shape[0], windows.rest_pad_wide, HPAD), f32),
+        ((windows.batch_count, windows.cin_pad_wide, PAIRS), f32),
+        ((windows.batch_count, windows.rest_pad_wide, HPAD), f32),
+        ((windows.extras, windows.rest_pad_wide, HPAD), f32),
     ]
     return pl.pallas_call(
         partial(dense_kernel, micro_count, windows),
-        in_specs=[in_smem] + [in_vmem] * 7,
+        in_specs=[in_smem] + [in_vmem] * 6,
         out_specs=[in_vmem] * len(shapes),
         out_shape=[jax.ShapeDtypeStruct(*shape) for shape in shapes],
         scratch_shapes=[
@@ -1158,7 +1182,7 @@
         ],
         compiler_params=pltpu.CompilerParams(vmem_limit_bytes=vmem_limit(windows.batch_count)),
         name="dense",
-    )(tower_at.reshape(1), stats, pooled, labels, weights, cins, rests, extras)
+    )(tower_at.reshape(1), stats, pooled, labels, weights, cin_full, rest_full)
 
 
 def shards(
@@ -1210,11 +1234,11 @@
         lanes_of(shard_ids), lanes_of(local_rows), lanes_of(bag_counts), sample_weights,
         slots, batch_count,
     )
-    pooled, served, stats, cins, rests, extras = fetch(
+    pooled, served, stats, cin_full, rest_full = fetch(
         requests, codes, halves, embed_table, cin_window, rest_window, windows, slots
     )
     grad_bags, loss, g_cins, g_rests, g_extras = dense_step(
-        tower_at, stats, pooled, click_labels, sample_weights, cins, rests, extras, windows
+        tower_at, stats, pooled, click_labels, sample_weights, cin_full, rest_full, windows
     )
     table_grad, losses, g_cin, g_rest = return_grads(
         grad_bags, codes, halves, served, loss, g_cins, g_rests, g_extras, windows, slots, columns

time: 179 us -> 176 us (0.983)
  Pallas kernels: 164 us -> 162 us
where the time goes in v4:
time: 176 us; the launch traced here: 175 us
  Pallas kernels  162 us (92%)
  other arithmetic  5.77 us (3%)
  local copies, waits for them, and re-layouts  3.91 us (2%)
  between operations  3.35 us (2%)
    pallas_call x1, Pallas kernels, fetch(): pl.pallas_call(partial(fetch_kernel, slots, windows, columns), in_specs=[...  67.6 us
    pallas_call x1, Pallas kernels, return_grads(): pl.pallas_call(partial(return_kernel, slots, windows, columns), in_specs=...  62.5 us
    pallas_call x1, Pallas kernels, route(): pl.pallas_call(partial(route_kernel, slots, batch_count), grid=(micro_cou...  19.4 us
    pallas_call x1, Pallas kernels, dense_step(): pl.pallas_call(partial(dense_kernel, micro_count, windows), in_specs=[in_...  12.2 us
    convert_element_type x1, other arithmetic, shards(): table_new.astype(jnp.bfloat16)  4.04 us

profile of v4, /device:TPU:0, one launch (start us, length us, event | category | flops | bytes accessed | tf_op | source)
XLA Modules:
  0.0 174.6 jit_solution(2702291244753417707)
XLA Ops:
  0.6 0.0 copy-start
  0.7 0.7 copy-done
  1.3 19.4 %route.1 = (s32[16,14,256]{2,1,0:T(8,128)S(1)}, s32[16,13,256]{2,1,0:T(8,128)S(1)}, s32[16,13,256]{2,1,0:T(8,128)S(1)}) custom-call(s32[3,80,104]{2,1,0:T(8,128)} %bitcast.15, s32[3,80,104]{2,1,0:T(8,128)} %bitcast.16, s32[3,39,104]{2,1,0:T(8,128)} %bitcast.17, s32[3,104]{1,0:T(4,128)S(1)} %copy-done), custom_call_target="tpu_custom_call" | custom-call | tf_op jit(solution)/shard_map/route/pallas_call | solution.py:246
  20.7 0.9 convert_element_type.13
  21.6 0.5 dynamic_update_slice.6
  22.2 0.2 reshape.49
  22.5 0.1 reshape.50.cin_ref
  22.6 0.5 dynamic_update_slice.7
  23.2 0.1 reshape.51
  23.3 67.6 %fetch.1 = (f32[3,248,256]{2,1,0:T(8,128)S(1)}, s32[16,14,256]{2,1,0:T(8,128)S(1)}, f32[8,128]{1,0:T(8,128)S(1)}, f32[208,1560]{1,0:T(8,128)S(1)}, f32[4,800,128]{2,1,0:T(8,128)S(1)}) custom-call(s32[16,14,256]{2,1,0:T(8,128)S(1)} %get-tuple-element.26.req_ref, s32[16,13,256]{2,1,0:T(8,128)S(1)} %get-tuple-element.27.code_ref, ...), custom_call_target="tpu_custom_call" | custom-call | tf_op jit(solution)/shard_map/fetch/pallas_call | solution.py:640
  90.9 0.0 copy-done.1
  90.9 0.0 copy-done.2
  90.9 0.0 copy-start.5
  91.0 12.2 %dense.1 = (bf16[3,248,256]{2,1,0:T(8,128)(2,1)S(1)}, f32[8,128]{1,0:T(8,128)S(1)}, f32[16,16,1560]{2,1,0:T(8,128)S(1)}, f32[16,56,512]{2,1,0:T(8,128)S(1)}, f32[1,56,512]{2,1,0:T(8,128)S(1)}) custom-call(s32[1]{0:T(128)} %bitcast.tower_ref, f32[8,128]{1,0:T(8,128)S(1)} %get-tuple-element.29.stat_ref, f32[3,248,256]{2,1,0:T(8,128)S(1)} %get-tuple-element.30.pooled_ref, ...), custom_call_target="tpu_custom_call" | custom-call | tf_op jit(solution)/shard_map/dense/pallas_call | solution.py:1169
  103.1 0.0 copy-start.3
  103.2 0.0 copy-start.4
  103.2 62.5 %return_grads.1 = (f32[11,32768]{1,0:T(8,128)S(1)}, f32[8,128]{1,0:T(8,128)S(1)}, f32[16,1560]{1,0:T(8,128)S(1)}, f32[56,512]{1,0:T(8,128)S(1)}) custom-call(bf16[3,248,256]{2,1,0:T(8,128)(2,1)S(1)} %get-tuple-element.33.grad_ref, s32[16,13,256]{2,1,0:T(8,128)S(1)} %get-tuple-element.27.code_ref, s32[16,13,256]{2,1,0:T(8,128)S(1)} %get-tuple-element.28.half_ref, ...), custom_call_target="tpu_custom_call" | custom-call | tf_op jit(solution)/shard_map/return_grads/pallas_call | solution.py:922
  165.6 0.0 copy-done.5
  165.6 0.0 copy-done.3
  165.6 0.0 copy-done.4
  165.7 0.0 copy-start.6
  165.7 0.0 copy-start.7
  165.7 0.0 copy-start.8
  165.7 4.0 %fusion.4 = (bf16[11,32768]{1,0:T(8,128)(2,1)}, f32[11,32768]{1,0:T(8,128)}, f32[11,32768]{1,0:T(8,128)}, f32[11,32768]{1,0:T(8,128)}) fusion(f32[11,32768]{1,0:T(8,128)S(1)} %copy-done.3, f32[11,32768]{1,0:T(8,128)S(1)} %get-tuple-element.39, f32[11,32768]{1,0:T(8,128)S(1)} %copy-done.4, f32[11,32768]{1,0:T(8,128)S(1)} %copy-done.5), kind=kLoop, calls=%fused_computation.11 | loop fusion | flops 5767168 | bytes 10813440 | tf_op jit(solution)/shard_map/convert_element_type | solution.py:1266
  169.7 0.1 reshape.54
  169.9 0.2 reshape.52
  170.0 0.2 reshape.53
  170.2 0.0 copy-done.6
  170.3 0.0 copy-done.7
  170.3 0.8 fusion.2
  171.1 0.5 slice.18
  171.6 0.5 slice.19
  (7 shorter events, 0.1 us)
Async XLA Ops:
  0.6 0.7 copy-start
  21.6 69.3 %copy-start.1 = (s32[3,104]{1,0:T(4,128)S(1)}, s32[3,104]{1,0:T(4,128)}, u32[]{:S(2)}) copy-start(s32[3,104]{1,0:T(4,128)} %weight_ref.3) | copy-start | bytes 3748
  21.6 69.3 %copy-start.2 = (s32[3,104]{1,0:T(4,128)S(1)}, s32[3,104]{1,0:T(4,128)}, u32[]{:S(2)}) copy-start(s32[3,104]{1,0:T(4,128)} %label_ref.1) | copy-start | bytes 3748
  90.9 74.7 %copy-start.5 = (f32[11,32768]{1,0:T(8,128)S(1)}, f32[11,32768]{1,0:T(8,128)}, u32[]{:S(2)}) copy-start(f32[11,32768]{1,0:T(8,128)} %param.18) | copy-start | bytes 4325380
  103.1 62.5 %copy-start.3 = (f32[11,32768]{1,0:T(8,128)S(1)}, f32[11,32768]{1,0:T(8,128)}, u32[]{:S(2)}) copy-start(f32[11,32768]{1,0:T(8,128)} %table_hbm_ref.1) | copy-start | bytes 4325380
  103.2 62.5 %copy-start.4 = (f32[11,32768]{1,0:T(8,128)S(1)}, f32[11,32768]{1,0:T(8,128)}, u32[]{:S(2)}) copy-start(f32[11,32768]{1,0:T(8,128)} %param.17) | copy-start | bytes 4325380
  165.7 4.6 %copy-start.6 = (f32[19426]{0:T(1024)S(1)}, f32[19426]{0:T(1024)}, u32[]{:S(2)}) copy-start(f32[19426]{0:T(1024)} %param.19) | copy-start | bytes 233116
  165.7 4.6 %copy-start.7 = (f32[19426]{0:T(1024)S(1)}, f32[19426]{0:T(1024)}, u32[]{:S(2)}) copy-start(f32[19426]{0:T(1024)} %param.20) | copy-start | bytes 233116
  165.7 4.6 %copy-start.8 = (f32[19426]{0:T(1024)S(1)}, f32[19426]{0:T(1024)}, u32[]{:S(2)}) copy-start(f32[19426]{0:T(1024)} %param.21) | copy-start | bytes 233116

commit v5 on v4

--- a/solution.py
+++ b/solution.py
@@ -29,6 +29,7 @@
 BAG_ROWS = EMB * HALF + 8
 FPAD = 40
 PAIRS = FIELDS * FPAD
+PAIRS_PAD = -(-PAIRS // LANES) * LANES
 SQUARE = FIELDS * FIELDS
 CIN_SIZE = MAPS * SQUARE + MAPS
 FLAT = EMB * FIELDS
@@ -107,6 +108,9 @@
         ]
         depth = batch_count // PLANE
         self.slots = [b % PLANE * depth + b // PLANE for b in range(batch_count)]
+        self.extra_skip = [max(0, -at) for at in self.extra_at]
+        longest = max(self.rest_rows - skip for skip in self.extra_skip)
+        self.extra_pad_wide = -(-longest // 8) * 8
         self.cin_total = -(-max(a + self.cin_rows for a in self.cin_at) // 8) * 8
         self.rest_total = -(-max(a + self.rest_rows for a in self.rest_at) // 8) * 8
 
@@ -203,7 +207,7 @@
         right_ref[:, span] = ones_at(iota((WIDE, LANES), 0).astype(f32) == row(1))
         return carry
 
-    lax.fori_loop(0, id_rows, build, 0, unroll=4)
+    lax.fori_loop(0, id_rows, build, 0, unroll=2)
     placed = dot(left_ref[...], right_ref[...], NT).astype(jnp.int32)
 
     def part(v, r):
@@ -256,7 +260,7 @@
         ],
         compiler_params=pltpu.CompilerParams(vmem_limit_bytes=vmem_limit(batch_count)),
         name="route",
-    )(in_hbm(ids), in_hbm(rows), in_hbm(counts), weights)
+    )(in_hbm(ids), in_hbm(rows), in_hbm(counts), in_hbm(weights))
 
 
 def peer_copy(src, dst, send_sem, recv_sem, peer):
@@ -612,7 +616,7 @@
     cin_full_ref[...] = jnp.zeros_like(cin_full_ref)
     for b, at in enumerate(windows.cin_at):
         block = cins_ref[windows.slots[b]].astype(jnp.float32)
-        cin_full_ref[at : at + windows.cin_rows, :] += block[: windows.cin_rows]
+        cin_full_ref[at : at + windows.cin_rows, :] += block[: windows.cin_rows, :PAIRS]
     rest_full_ref[...] = jnp.zeros_like(rest_full_ref)
     pieces = [(rests_ref, windows.slots[b], at) for b, at in enumerate(windows.rest_at)]
     pieces += [(extras_ref, e, at) for e, at in enumerate(windows.extra_at)]
@@ -833,7 +837,7 @@
             def _():
                 split(start_windows)
 
-            @pl.when((j == 1) & (tower == 0))
+            @pl.when((j == 3) & (tower == 0))
             def _():
                 for e in range(windows.extras):
 
@@ -875,6 +879,7 @@
 
     @pl.when(tower == 0)
     def _():
+        rest_ref[...] = jnp.zeros_like(rest_ref)
         for e in range(windows.extras):
 
             @pl.when(me != first_extra + e)
@@ -885,11 +890,12 @@
         def _():
             extra_in_ref[me] = extras_ref[me - first_extra]
             others(lambda peer: extra_copy(me, peer).wait_recv())
-            rest_ref[...] = jnp.sum(extra_in_ref[...], axis=0)
-
-        @pl.when(me < first_extra)
-        def _():
-            rest_ref[...] = jnp.zeros_like(rest_ref)
+            total = jnp.sum(extra_in_ref[...], axis=0)
+            for e, skip in enumerate(windows.extra_skip):
+
+                @pl.when(me == first_extra + e)
+                def _():
+                    rest_ref[skip : windows.rest_rows, :] = total[: windows.rest_rows - skip]
 
     @pl.when(tower == 1)
     def _():
@@ -937,7 +943,7 @@
             pltpu.VMEM((columns * TALL, long), jnp.bfloat16),
             pltpu.VMEM((BROAD, long), jnp.bfloat16),
             pltpu.VMEM((columns * TALL, BROAD), jnp.float32),
-            pltpu.VMEM(rests.shape, jnp.float32),
+            pltpu.VMEM((batch_count,) + extras.shape[1:], jnp.float32),
         ]
         + [
             pltpu.VMEM(lead + x.shape[1:], jnp.float32)
@@ -1085,7 +1091,7 @@
             return total + sym_ref[here, :] * embed_ref[pl.ds(d * FPAD + j, 1), :]
 
         grad_embed = lax.fori_loop(
-            0, FIELDS, add_row, grad_flat[d * FPAD : (d + 1) * FPAD], unroll=13
+            0, FIELDS, add_row, grad_flat[d * FPAD : (d + 1) * FPAD], unroll=39
         )
         grad_embed = jnp.concatenate([grad_embed, empty], axis=0)
         for m in range(micro_count):
@@ -1126,14 +1132,14 @@
         thirds_u = split_three(jnp.broadcast_to(g_cin_u, (MAPS, 8)))
         g_cin_ref[MAPS : MAPS + 1, :] = sum(dot(third, picks_u, TN) for third in thirds_u)[:1]
         for b, at in enumerate(windows.cin_at):
-            g_cins_ref[windows.slots[b], : windows.cin_rows, :] = g_cin_ref[
+            g_cins_ref[windows.slots[b], : windows.cin_rows, :PAIRS] = g_cin_ref[
                 at : at + windows.cin_rows, :
             ]
         for e, at in enumerate(windows.extra_at):
             skip = max(0, -at)
             for l in range(groups):
                 span = slice(l * LANES, (l + 1) * LANES)
-                g_extras_ref[e, skip : windows.rest_rows, span] = g_rest_ref[
+                g_extras_ref[e, : windows.rest_rows - skip, span] = g_rest_ref[
                     l, at + skip : at + windows.rest_rows, :
                 ]
 
@@ -1162,9 +1168,9 @@
     shapes = [
         ((micro_count, BAG_ROWS, WIDE), jnp.bfloat16),
         ((8, LANES), f32),
-        ((windows.batch_count, windows.cin_pad_wide, PAIRS), f32),
+        ((windows.batch_count, windows.cin_pad_wide, PAIRS_PAD), f32),
         ((windows.batch_count, windows.rest_pad_wide, HPAD), f32),
-        ((windows.extras, windows.rest_pad_wide, HPAD), f32),
+        ((windows.extras, windows.extra_pad_wide, HPAD), f32),
     ]
     return pl.pallas_call(
         partial(dense_kernel, micro_count, windows),
@@ -1222,6 +1228,7 @@
         cin_window,
         ((0, windows.cin_pad - windows.cin_rows), (0, 0), (0, FPAD - FIELDS)),
     ).reshape(windows.cin_pad, PAIRS)
+    cin_window = jnp.pad(cin_window, ((0, 0), (0, PAIRS_PAD - PAIRS)))
     rest_window = jnp.pad(
         window(windows.rest_rows, HID, rest_phase).reshape(-1, HID),
         ((0, windows.rest_pad - windows.rest_rows), (0, HPAD - HID)),
@@ -1243,7 +1250,7 @@
     table_grad, losses, g_cin, g_rest = return_grads(
         grad_bags, codes, halves, served, loss, g_cins, g_rests, g_extras, windows, slots, columns
     )
-    g_cin = g_cin[: windows.cin_rows].reshape(-1, FIELDS, FPAD)[:, :, :FIELDS].reshape(-1)
+    g_cin = g_cin[: windows.cin_rows, :PAIRS].reshape(-1, FIELDS, FPAD)[:, :, :FIELDS].reshape(-1)
     g_rest = g_rest[: windows.rest_rows, :HID].reshape(-1)
     is_cin = device * share + jnp.arange(share, dtype=jnp.int32) < CIN_SIZE
     own_grad = jnp.where(

time: 176 us -> 174 us (0.989)
  no operation moved by 1% of the time
where the time goes in v5:
time: 174 us; the launch traced here: 173 us
  Pallas kernels  161 us (93%)
  other arithmetic  5.77 us (3%)
  between operations  3.29 us (2%)
  local copies, waits for them, and re-layouts  3.21 us (2%)
    pallas_call x1, Pallas kernels, fetch(): pl.pallas_call(partial(fetch_kernel, slots, windows, columns), in_specs=[...  67.6 us
    pallas_call x1, Pallas kernels, return_grads(): pl.pallas_call(partial(return_kernel, slots, windows, columns), in_specs=...  62.7 us
    pallas_call x1, Pallas kernels, route(): pl.pallas_call(partial(route_kernel, slots, batch_count), grid=(micro_cou...  19 us
    pallas_call x1, Pallas kernels, dense_step(): pl.pallas_call(partial(dense_kernel, micro_count, windows), in_specs=[in_...  11.4 us
    convert_element_type x1, other arithmetic, shards(): table_new.astype(jnp.bfloat16)  4.04 us

profile of v5, /device:TPU:0, one launch (start us, length us, event | category | flops | bytes accessed | tf_op | source)
XLA Modules:
  0.0 173.0 jit_solution(2886523061858901984)
XLA Ops:
  0.6 19.0 %route.1 = (s32[16,14,256]{2,1,0:T(8,128)S(1)}, s32[16,13,256]{2,1,0:T(8,128)S(1)}, s32[16,13,256]{2,1,0:T(8,128)S(1)}) custom-call(s32[3,80,104]{2,1,0:T(8,128)} %bitcast.15, s32[3,80,104]{2,1,0:T(8,128)} %bitcast.16, s32[3,39,104]{2,1,0:T(8,128)} %bitcast.17, s32[3,104]{1,0:T(4,128)} %weight_ref.3), custom_call_target="tpu_custom_call" | custom-call | tf_op jit(solution)/shard_map/route/pallas_call | solution.py:250
  19.7 0.9 convert_element_type.15
  20.6 0.5 dynamic_update_slice.6
  21.1 0.0 copy-start
  21.2 0.0 copy-start.1
  21.2 0.2 reshape.49
  21.4 0.1 reshape.50
  21.6 0.5 dynamic_update_slice.7
  22.2 0.1 reshape.51
  22.3 67.6 %fetch.1 = (f32[3,248,256]{2,1,0:T(8,128)S(1)}, s32[16,14,256]{2,1,0:T(8,128)S(1)}, f32[8,128]{1,0:T(8,128)S(1)}, f32[208,1560]{1,0:T(8,128)S(1)}, f32[4,800,128]{2,1,0:T(8,128)S(1)}) custom-call(s32[16,14,256]{2,1,0:T(8,128)S(1)} %get-tuple-element.26.req_ref, s32[16,13,256]{2,1,0:T(8,128)S(1)} %get-tuple-element.27.code_ref, ...), custom_call_target="tpu_custom_call" | custom-call | tf_op jit(solution)/shard_map/fetch/pallas_call | solution.py:644
  89.9 0.0 copy-done
  89.9 0.0 copy-done.1
  89.9 0.0 copy-start.4
  89.9 11.4 %dense.1 = (bf16[3,248,256]{2,1,0:T(8,128)(2,1)S(1)}, f32[8,128]{1,0:T(8,128)S(1)}, f32[16,16,1664]{2,1,0:T(8,128)S(1)}, f32[16,56,512]{2,1,0:T(8,128)S(1)}, f32[1,24,512]{2,1,0:T(8,128)S(1)}) custom-call(s32[1]{0:T(128)} %bitcast.tower_ref, f32[8,128]{1,0:T(8,128)S(1)} %get-tuple-element.29.stat_ref, f32[3,248,256]{2,1,0:T(8,128)S(1)} %get-tuple-element.30.pooled_ref, ...), custom_call_target="tpu_custom_call" | custom-call | tf_op jit(solution)/shard_map/dense/pallas_call | solution.py:1175
  101.3 0.0 copy-start.2
  101.3 0.0 copy-start.3
  101.3 62.7 %return_grads.1 = (f32[11,32768]{1,0:T(8,128)S(1)}, f32[8,128]{1,0:T(8,128)S(1)}, f32[16,1664]{1,0:T(8,128)S(1)}, f32[56,512]{1,0:T(8,128)S(1)}) custom-call(bf16[3,248,256]{2,1,0:T(8,128)(2,1)S(1)} %get-tuple-element.33.grad_ref, s32[16,13,256]{2,1,0:T(8,128)S(1)} %get-tuple-element.27.code_ref, s32[16,13,256]{2,1,0:T(8,128)S(1)} %get-tuple-element.28.half_ref, ...), custom_call_target="tpu_custom_call" | custom-call | tf_op jit(solution)/shard_map/return_grads/pallas_call | solution.py:928
  164.1 0.0 copy-done.4
  164.1 0.0 copy-done.2
  164.1 0.0 copy-start.5
  164.1 0.0 copy-start.6
  164.1 0.0 copy-start.7
  164.1 4.0 %fusion.4 = (bf16[11,32768]{1,0:T(8,128)(2,1)}, f32[11,32768]{1,0:T(8,128)}, f32[11,32768]{1,0:T(8,128)}, f32[11,32768]{1,0:T(8,128)}) fusion(f32[11,32768]{1,0:T(8,128)S(1)} %copy-done.2, f32[11,32768]{1,0:T(8,128)S(1)} %get-tuple-element.39, f32[11,32768]{1,0:T(8,128)S(1)} %copy-done.3, f32[11,32768]{1,0:T(8,128)S(1)} %copy-done.4), kind=kLoop, calls=%fused_computation.11 | loop fusion | flops 5767168 | bytes 10813440 | tf_op jit(solution)/shard_map/convert_element_type | solution.py:1273
  168.2 0.1 reshape.54
  168.3 0.2 reshape.52
  168.5 0.2 reshape.53
  168.7 0.0 copy-done.5
  168.7 0.0 copy-done.6
  168.7 0.0 copy-done.7
  168.7 0.8 fusion.2
  169.5 0.5 slice.18
  170.1 0.5 slice.19
  (6 shorter events, 0.1 us)
Async XLA Ops:
  21.1 68.8 %copy-start = (s32[3,104]{1,0:T(4,128)S(1)}, s32[3,104]{1,0:T(4,128)}, u32[]{:S(2)}) copy-start(s32[3,104]{1,0:T(4,128)} %weight_ref.3) | copy-start | bytes 3748
  21.2 68.8 %copy-start.1 = (s32[3,104]{1,0:T(4,128)S(1)}, s32[3,104]{1,0:T(4,128)}, u32[]{:S(2)}) copy-start(s32[3,104]{1,0:T(4,128)} %label_ref.1) | copy-start | bytes 3748
  89.9 74.1 %copy-start.4 = (f32[11,32768]{1,0:T(8,128)S(1)}, f32[11,32768]{1,0:T(8,128)}, u32[]{:S(2)}) copy-start(f32[11,32768]{1,0:T(8,128)} %param.18) | copy-start | bytes 4325380
  101.3 62.8 %copy-start.2 = (f32[11,32768]{1,0:T(8,128)S(1)}, f32[11,32768]{1,0:T(8,128)}, u32[]{:S(2)}) copy-start(f32[11,32768]{1,0:T(8,128)} %table_hbm_ref.1) | copy-start | bytes 4325380
  101.3 62.8 %copy-start.3 = (f32[11,32768]{1,0:T(8,128)S(1)}, f32[11,32768]{1,0:T(8,128)}, u32[]{:S(2)}) copy-start(f32[11,32768]{1,0:T(8,128)} %param.17) | copy-start | bytes 4325380
  164.1 4.6 %copy-start.5 = (f32[19426]{0:T(1024)S(1)}, f32[19426]{0:T(1024)}, u32[]{:S(2)}) copy-start(f32[19426]{0:T(1024)} %param.19) | copy-start | bytes 233116
  164.1 4.6 %copy-start.6 = (f32[19426]{0:T(1024)S(1)}, f32[19426]{0:T(1024)}, u32[]{:S(2)}) copy-start(f32[19426]{0:T(1024)} %param.20) | copy-start | bytes 233116
  164.1 4.6 %copy-start.7 = (f32[19426]{0:T(1024)S(1)}, f32[19426]{0:T(1024)}, u32[]{:S(2)}) copy-start(f32[19426]{0:T(1024)} %param.21) | copy-start | bytes 233116

commit v6 on v5

--- a/solution.py
+++ b/solution.py
@@ -510,7 +510,7 @@
             pair_copy(rests_ref, rests_ref, 0).start()
 
     pairs = batch_count // 2
-    lag = 2
+    lag = 3
 
     last = lax.rem(me + 1, batch_count)
 
@@ -1081,7 +1081,7 @@
         sym_ref[here, :] = jnp.concatenate(both, axis=1)
         return carry
 
-    lax.fori_loop(0, FIELDS, mirror, 0, unroll=3)
+    lax.fori_loop(0, FIELDS, mirror, 0, unroll=13)
     empty = jnp.zeros((2 * HALF - FPAD, width), f32)
 
     for d in range(EMB):

time: 174 us -> 173 us (level)
  Pallas kernels: 161 us -> 159 us
where the time goes in v6:
time: 173 us; the launch traced here: 172 us
  Pallas kernels  159 us (92%)
  other arithmetic  5.77 us (3%)
  between operations  3.29 us (2%)
  local copies, waits for them, and re-layouts  3.21 us (2%)
    pallas_call x1, Pallas kernels, fetch(): pl.pallas_call(partial(fetch_kernel, slots, windows, columns), in_specs=[...  66.5 us
    pallas_call x1, Pallas kernels, return_grads(): pl.pallas_call(partial(return_kernel, slots, windows, columns), in_specs=...  62.7 us
    pallas_call x1, Pallas kernels, route(): pl.pallas_call(partial(route_kernel, slots, batch_count), grid=(micro_cou...  19 us
    pallas_call x1, Pallas kernels, dense_step(): pl.pallas_call(partial(dense_kernel, micro_count, windows), in_specs=[in_...  11.3 us
    convert_element_type x1, other arithmetic, shards(): table_new.astype(jnp.bfloat16)  4.04 us

profile of v6, /device:TPU:0, one launch (start us, length us, event | category | flops | bytes accessed | tf_op | source)
XLA Modules:
  0.0 171.7 jit_solution(8084995625432450343)
XLA Ops:
  0.6 19.0 %route.1 = (s32[16,14,256]{2,1,0:T(8,128)S(1)}, s32[16,13,256]{2,1,0:T(8,128)S(1)}, s32[16,13,256]{2,1,0:T(8,128)S(1)}) custom-call(s32[3,80,104]{2,1,0:T(8,128)} %bitcast.15, s32[3,80,104]{2,1,0:T(8,128)} %bitcast.16, s32[3,39,104]{2,1,0:T(8,128)} %bitcast.17, s32[3,104]{1,0:T(4,128)} %weight_ref.3), custom_call_target="tpu_custom_call" | custom-call | tf_op jit(solution)/shard_map/route/pallas_call | solution.py:250
  19.7 0.9 convert_element_type.15
  20.6 0.5 dynamic_update_slice.6
  21.1 0.0 copy-start
  21.2 0.0 copy-start.1
  21.2 0.2 reshape.49
  21.4 0.1 reshape.50
  21.6 0.5 dynamic_update_slice.7
  22.2 0.1 reshape.51
  22.3 66.5 %fetch.1 = (f32[3,248,256]{2,1,0:T(8,128)S(1)}, s32[16,14,256]{2,1,0:T(8,128)S(1)}, f32[8,128]{1,0:T(8,128)S(1)}, f32[208,1560]{1,0:T(8,128)S(1)}, f32[4,800,128]{2,1,0:T(8,128)S(1)}) custom-call(s32[16,14,256]{2,1,0:T(8,128)S(1)} %get-tuple-element.26.req_ref, s32[16,13,256]{2,1,0:T(8,128)S(1)} %get-tuple-element.27.code_ref, ...), custom_call_target="tpu_custom_call" | custom-call | tf_op jit(solution)/shard_map/fetch/pallas_call | solution.py:644
  88.8 0.0 copy-done
  88.8 0.0 copy-done.1
  88.8 0.0 copy-start.4
  88.8 11.3 %dense.1 = (bf16[3,248,256]{2,1,0:T(8,128)(2,1)S(1)}, f32[8,128]{1,0:T(8,128)S(1)}, f32[16,16,1664]{2,1,0:T(8,128)S(1)}, f32[16,56,512]{2,1,0:T(8,128)S(1)}, f32[1,24,512]{2,1,0:T(8,128)S(1)}) custom-call(s32[1]{0:T(128)} %bitcast.tower_ref, f32[8,128]{1,0:T(8,128)S(1)} %get-tuple-element.29.stat_ref, f32[3,248,256]{2,1,0:T(8,128)S(1)} %get-tuple-element.30.pooled_ref, ...), custom_call_target="tpu_custom_call" | custom-call | tf_op jit(solution)/shard_map/dense/pallas_call | solution.py:1175
  100.1 0.0 copy-start.2
  100.1 0.0 copy-start.3
  100.1 62.7 %return_grads.1 = (f32[11,32768]{1,0:T(8,128)S(1)}, f32[8,128]{1,0:T(8,128)S(1)}, f32[16,1664]{1,0:T(8,128)S(1)}, f32[56,512]{1,0:T(8,128)S(1)}) custom-call(bf16[3,248,256]{2,1,0:T(8,128)(2,1)S(1)} %get-tuple-element.33.grad_ref, s32[16,13,256]{2,1,0:T(8,128)S(1)} %get-tuple-element.27.code_ref, s32[16,13,256]{2,1,0:T(8,128)S(1)} %get-tuple-element.28.half_ref, ...), custom_call_target="tpu_custom_call" | custom-call | tf_op jit(solution)/shard_map/return_grads/pallas_call | solution.py:928
  162.9 0.0 copy-done.4
  162.9 0.0 copy-done.2
  162.9 0.0 copy-done.3
  162.9 0.0 copy-start.5
  162.9 0.0 copy-start.6
  162.9 0.0 copy-start.7
  162.9 4.0 %fusion.4 = (bf16[11,32768]{1,0:T(8,128)(2,1)}, f32[11,32768]{1,0:T(8,128)}, f32[11,32768]{1,0:T(8,128)}, f32[11,32768]{1,0:T(8,128)}) fusion(f32[11,32768]{1,0:T(8,128)S(1)} %copy-done.2, f32[11,32768]{1,0:T(8,128)S(1)} %get-tuple-element.39, f32[11,32768]{1,0:T(8,128)S(1)} %copy-done.3, f32[11,32768]{1,0:T(8,128)S(1)} %copy-done.4), kind=kLoop, calls=%fused_computation.11 | loop fusion | flops 5767168 | bytes 10813440 | tf_op jit(solution)/shard_map/convert_element_type | solution.py:1273
  167.0 0.1 reshape.54
  167.1 0.2 reshape.52
  167.2 0.2 reshape.53
  167.5 0.0 copy-done.5
  167.5 0.0 copy-done.6
  167.5 0.8 fusion.2
  168.3 0.5 slice.18
  168.8 0.5 slice.19
  (6 shorter events, 0.1 us)
Async XLA Ops:
  21.1 67.7 %copy-start = (s32[3,104]{1,0:T(4,128)S(1)}, s32[3,104]{1,0:T(4,128)}, u32[]{:S(2)}) copy-start(s32[3,104]{1,0:T(4,128)} %weight_ref.3) | copy-start | bytes 3748
  21.2 67.7 %copy-start.1 = (s32[3,104]{1,0:T(4,128)S(1)}, s32[3,104]{1,0:T(4,128)}, u32[]{:S(2)}) copy-start(s32[3,104]{1,0:T(4,128)} %label_ref.1) | copy-start | bytes 3748
  88.8 74.0 %copy-start.4 = (f32[11,32768]{1,0:T(8,128)S(1)}, f32[11,32768]{1,0:T(8,128)}, u32[]{:S(2)}) copy-start(f32[11,32768]{1,0:T(8,128)} %param.18) | copy-start | bytes 4325380
  100.1 62.8 %copy-start.2 = (f32[11,32768]{1,0:T(8,128)S(1)}, f32[11,32768]{1,0:T(8,128)}, u32[]{:S(2)}) copy-start(f32[11,32768]{1,0:T(8,128)} %table_hbm_ref.1) | copy-start | bytes 4325380
  100.1 62.7 %copy-start.3 = (f32[11,32768]{1,0:T(8,128)S(1)}, f32[11,32768]{1,0:T(8,128)}, u32[]{:S(2)}) copy-start(f32[11,32768]{1,0:T(8,128)} %param.17) | copy-start | bytes 4325380
  162.9 4.6 %copy-start.5 = (f32[19426]{0:T(1024)S(1)}, f32[19426]{0:T(1024)}, u32[]{:S(2)}) copy-start(f32[19426]{0:T(1024)} %param.19) | copy-start | bytes 233116
  162.9 4.6 %copy-start.6 = (f32[19426]{0:T(1024)S(1)}, f32[19426]{0:T(1024)}, u32[]{:S(2)}) copy-start(f32[19426]{0:T(1024)} %param.20) | copy-start | bytes 233116
  162.9 4.6 %copy-start.7 = (f32[19426]{0:T(1024)S(1)}, f32[19426]{0:T(1024)}, u32[]{:S(2)}) copy-start(f32[19426]{0:T(1024)} %param.21) | copy-start | bytes 233116
